TPU v7x, 128 devices: a whole 4x4x4 slice. The times are simulated.
128 devices in a mesh: expert: 128 (over x, z, y, core).
Axes of the slice: x: 4, y: 4, z: 4, core: 2. Of those that a mesh axis runs over, the one named last changes fastest.
Arguments:
- routed_rows: bfloat16 [24576, 2048], P('expert'), may hold values from -6 to 6
- expert_index: int32 [24576, 1], P('expert'), may hold values from 0 to 127; in each aligned block of 192 rows (0 to 191, 192 to 383, ...) at most 3 rows name the same one
- route_weight: float32 [24576], P('expert'), may hold values from 0.1 to 1
- cotangent: bfloat16 [24576, 2048], P('expert'), may hold values from -6 to 6
- gate_weight: bfloat16 [128, 2048, 768], P('expert'), may hold values from -0.125 to 0.125
- up_weight: bfloat16 [128, 2048, 768], P('expert'), may hold values from -0.125 to 0.125
- down_weight: bfloat16 [128, 768, 2048], P('expert'), may hold values from -0.21875 to 0.21875
Outputs:
- layer_out: bfloat16 [24576, 2048], P('expert')
- row_grad: bfloat16 [24576, 2048], P('expert')
- weight_grad: float32 [24576], P('expert')
- gate_grad: bfloat16 [128, 2048, 768], P('expert')
- up_grad: bfloat16 [128, 2048, 768], P('expert')
- down_grad: bfloat16 [128, 768, 2048], P('expert')
Inputs may be any that keep to these rules, and one draw needn't show every extreme that they name: `expert_index`: among the 192 rows of one device no expert is named more than 3 times, a bound that some block reaches.
All inputs are finite; a program needn't handle non-finite values.
Results may differ from a plain program's by a relative error of at most 0.0058.
Values may be sent and summed in bfloat16 or wider, within the bound.
No kernel may reach another device: no remote copies, remote signals or barrier semaphores. Data moves between devices by JAX's collectives and lax.ppermute only.
A program may use at most 128 MiB of HBM per device.

v0:
```python
import jax
import jax.numpy as jnp
from jax import lax
from jax.sharding import PartitionSpec as P


def forward_part(rows_in, w_gate, w_up, w_down):
    gate_act = jnp.dot(rows_in, w_gate, preferred_element_type=jnp.float32)
    up_act = jnp.dot(rows_in, w_up, preferred_element_type=jnp.float32)
    sigma = jax.nn.sigmoid(gate_act)
    silu_gate = gate_act * sigma
    hidden = (silu_gate * up_act).astype(jnp.bfloat16)
    expert_out = jnp.dot(hidden, w_down, preferred_element_type=jnp.float32).astype(jnp.bfloat16)
    return (expert_out, (gate_act, up_act, sigma, silu_gate, hidden))


def backward_part(rows_in, out_grad, saved, w_gate, w_up, w_down):
    gate_act, up_act, sigma, silu_gate, hidden = saved
    hidden_grad = lax.dot_general(
        out_grad, w_down, (((1,), (1,)), ((), ())), preferred_element_type=jnp.float32
    )
    gate_pre = (hidden_grad * up_act * sigma * (1.0 + gate_act * (1.0 - sigma))).astype(
        jnp.bfloat16
    )
    up_pre = (hidden_grad * silu_gate).astype(jnp.bfloat16)
    input_grad = (
        lax.dot_general(
            gate_pre, w_gate, (((1,), (1,)), ((), ())), preferred_element_type=jnp.float32
        )
        + lax.dot_general(
            up_pre, w_up, (((1,), (1,)), ((), ())), preferred_element_type=jnp.float32
        )
    ).astype(jnp.bfloat16)
    gate_grad = lax.dot_general(
        rows_in, gate_pre, (((0,), (0,)), ((), ())), preferred_element_type=jnp.float32
    ).astype(jnp.bfloat16)
    up_grad = lax.dot_general(
        rows_in, up_pre, (((0,), (0,)), ((), ())), preferred_element_type=jnp.float32
    ).astype(jnp.bfloat16)
    down_grad = lax.dot_general(
        hidden, out_grad, (((0,), (0,)), ((), ())), preferred_element_type=jnp.float32
    ).astype(jnp.bfloat16)
    return (input_grad, gate_grad, up_grad, down_grad)


def local(routed_rows, expert_index, route_weight, cotangent, gate_weight, up_weight, down_weight):
    devices = lax.axis_size("expert")
    row_count = routed_rows.shape[0]
    width = routed_rows.shape[1]
    capacity = max(2, 2 * row_count // devices)
    choice_ids = expert_index[:, 0]
    onehot = (choice_ids[:, None] == jnp.arange(devices, dtype=jnp.int32)[None, :]).astype(
        jnp.float32
    )
    earlier = (jnp.arange(row_count)[:, None] > jnp.arange(row_count)[None, :]).astype(jnp.float32)
    before = jnp.dot(earlier, onehot, preferred_element_type=jnp.float32)
    rank_within = jnp.sum(before * onehot, axis=1).astype(jnp.int32)
    slot_index = choice_ids * capacity + rank_within
    scatter_table = (
        jnp.arange(devices * capacity, dtype=jnp.int32)[:, None] == slot_index[None, :]
    ).astype(jnp.bfloat16)
    out_grad = (route_weight[:, None] * cotangent.astype(jnp.float32)).astype(jnp.bfloat16)
    send_rows = jnp.dot(scatter_table, routed_rows, preferred_element_type=jnp.float32).astype(
        jnp.bfloat16
    )
    send_rows = send_rows.reshape(devices, capacity, width)
    send_grad = jnp.dot(scatter_table, out_grad, preferred_element_type=jnp.float32).astype(
        jnp.bfloat16
    )
    send_grad = send_grad.reshape(devices, capacity, width)
    w_gate = gate_weight[0]
    w_up = up_weight[0]
    w_down = down_weight[0]
    got_rows = lax.all_to_all(send_rows, "expert", split_axis=0, concat_axis=0, tiled=True)
    rows_in = got_rows.reshape(devices * capacity, width)
    expert_out, saved = forward_part(rows_in, w_gate, w_up, w_down)
    back_out = lax.all_to_all(
        expert_out.reshape(devices, capacity, width),
        "expert",
        split_axis=0,
        concat_axis=0,
        tiled=True,
    )
    got_grad = lax.all_to_all(send_grad, "expert", split_axis=0, concat_axis=0, tiled=True)
    input_grad, gate_grad, up_grad, down_grad = backward_part(
        rows_in, got_grad.reshape(devices * capacity, width), saved, w_gate, w_up, w_down
    )
    back_grad = lax.all_to_all(
        input_grad.reshape(devices, capacity, width),
        "expert",
        split_axis=0,
        concat_axis=0,
        tiled=True,
    )
    gather_dims = (((0,), (0,)), ((), ()))
    out_rows = lax.dot_general(
        scatter_table,
        back_out.reshape(devices * capacity, width),
        gather_dims,
        preferred_element_type=jnp.float32,
    ).astype(jnp.bfloat16)
    row_grad = lax.dot_general(
        scatter_table,
        back_grad.reshape(devices * capacity, width),
        gather_dims,
        preferred_element_type=jnp.float32,
    ).astype(jnp.bfloat16)
    layer_out = (route_weight[:, None] * out_rows.astype(jnp.float32)).astype(jnp.bfloat16)
    weight_grad = jnp.sum(cotangent.astype(jnp.float32) * out_rows.astype(jnp.float32), axis=1)
    return (layer_out, row_grad, weight_grad, gate_grad[None], up_grad[None], down_grad[None])


def solution(mesh):
    return jax.shard_map(
        local,
        mesh=mesh,
        in_specs=(
            P("expert", None),
            P("expert", None),
            P("expert"),
            P("expert", None),
            P("expert", None, None),
            P("expert", None, None),
            P("expert", None, None),
        ),
        out_specs=(
            P("expert", None),
            P("expert", None),
            P("expert"),
            P("expert", None, None),
            P("expert", None, None),
            P("expert", None, None),
        ),
        check_vma=False,
    )
```

profile of v0, /device:TPU:1, one launch (start us, length us, event | category | flops | bytes accessed | tf_op | source)
XLA Modules:
  0.0 188.3 jit_solution(1182657986805188702)
XLA Ops:
  2.5 2.9 %convolution_convert_fusion.3 = bf16[384,2048]{1,0:T(8,128)(2,1)} fusion(bf16[192,2048]{1,0:T(8,128)(2,1)} %param.10, f32[192]{0:T(256)} %param.9, s32[192]{0:T(256)S(1)} %convert_add_fusion), kind=kOutput, calls=%fused_computation.20 | convolution fusion | flops 304029696 | bytes 2360832 | tf_op jit(solution)/shard_map/dot_general | solution.py:67
  5.4 5.2 %reshape.50 = bf16[128,3,2048]{2,1,0:T(4,128)(2,1)} reshape(bf16[384,2048]{1,0:T(8,128)(2,1)} %convolution_convert_fusion.3) | data formatting | bytes 3145728 | tf_op jit(solution)/shard_map/reshape | solution.py:70
  10.6 12.0 %all-to-all-start.2 = ((bf16[128,3,2048]{2,1,0:T(4,128)(2,1)}), bf16[128,3,2048]{2,1,0:T(4,128)(2,1)}, u32[]{:S(2)}, u32[]{:S(2)}) async-start(bf16[128,3,2048]{2,1,0:T(4,128)(2,1)} %reshape.50), calls=%async_computation.2 | async-start | bytes 4194304 | tf_op jit(solution)/shard_map/all_to_all | solution.py:84
  25.4 5.2 %reshape.46 = bf16[128,3,2048]{2,1,0:T(4,128)(2,1)} reshape(bf16[384,2048]{1,0:T(8,128)(2,1)} %convolution_convert_fusion.4) | data formatting | bytes 3145728 | tf_op jit(solution)/shard_map/reshape | solution.py:66
  30.6 22.0 %all-to-all-done.2 = bf16[128,3,2048]{2,1,0:T(4,128)(2,1)} async-done(((bf16[128,3,2048]{2,1,0:T(4,128)(2,1)}), bf16[128,3,2048]{2,1,0:T(4,128)(2,1)}, u32[]{:S(2)}, u32[]{:S(2)}) %all-to-all-start.2) | async-done | bytes 1572896 | tf_op jit(solution)/shard_map/all_to_all | solution.py:84
  52.6 5.6 %all-to-all-start = ((bf16[128,3,2048]{2,1,0:T(4,128)(2,1)}), bf16[128,3,2048]{2,1,0:T(4,128)(2,1)}, u32[]{:S(2)}, u32[]{:S(2)}) async-start(bf16[128,3,2048]{2,1,0:T(4,128)(2,1)} %reshape.46), calls=%async_computation | async-start | bytes 4194304 | tf_op jit(solution)/shard_map/all_to_all | solution.py:74
  58.2 5.0 %reshape.51 = bf16[384,2048]{1,0:T(8,128)(2,1)} reshape(bf16[128,3,2048]{2,1,0:T(4,128)(2,1)} %all-to-all-done.2) | data formatting | bytes 3145728 | tf_op jit(solution)/shard_map/reshape | solution.py:86
  63.3 4.8 %fusion = f32[384,768]{1,0:T(8,128)} fusion(bf16[384,2048]{1,0:T(8,128)(2,1)} %reshape.51, bf16[1,768,2048]{2,1,0:T(8,128)(2,1)} %param.13), kind=kOutput, calls=%fused_computation.3 | convolution fusion | flops 1207959552 | bytes 5898240 | tf_op jit(solution)/shard_map/dot_general | solution.py:19
  68.1 20.3 %all-to-all-done = bf16[128,3,2048]{2,1,0:T(4,128)(2,1)} async-done(((bf16[128,3,2048]{2,1,0:T(4,128)(2,1)}), bf16[128,3,2048]{2,1,0:T(4,128)(2,1)}, u32[]{:S(2)}, u32[]{:S(2)}) %all-to-all-start) | async-done | bytes 1572896 | tf_op jit(solution)/shard_map/all_to_all | solution.py:74
  88.4 5.0 %reshape.47 = bf16[384,2048]{1,0:T(8,128)(2,1)} reshape(bf16[128,3,2048]{2,1,0:T(4,128)(2,1)} %all-to-all-done) | data formatting | bytes 3145728 | tf_op jit(solution)/shard_map/reshape | solution.py:75
  93.4 3.9 %fusion.6 = f32[384,768]{1,0:T(8,128)S(1)} fusion(bf16[384,2048]{1,0:T(8,128)(2,1)} %reshape.47, bf16[1,2048,768]{2,1,0:T(8,128)(2,1)} %param.12), kind=kOutput, calls=%fused_computation.9 | convolution fusion | flops 1207959552 | bytes 5898240 | tf_op jit(solution)/shard_map/dot_general | solution.py:9
  103.6 5.2 %reshape.48 = bf16[128,3,2048]{2,1,0:T(4,128)(2,1)} reshape(bf16[384,2048]{1,0:T(8,128)(2,1)} %fusion.17) | data formatting | bytes 3145728 | tf_op jit(solution)/shard_map/reshape | solution.py:78
  108.8 5.6 %all-to-all-start.1 = ((bf16[128,3,2048]{2,1,0:T(4,128)(2,1)}), bf16[128,3,2048]{2,1,0:T(4,128)(2,1)}, u32[]{:S(2)}, u32[]{:S(2)}) async-start(bf16[128,3,2048]{2,1,0:T(4,128)(2,1)} %reshape.48), calls=%async_computation.1 | async-start | bytes 4194304 | tf_op jit(solution)/shard_map/all_to_all | solution.py:77
  114.4 3.5 %fusion.4 = f32[384,2048]{1,0:T(8,128)S(1)} fusion(bf16[384,768]{1,0:T(8,128)(2,1)} %get-tuple-element.7, bf16[1,2048,768]{2,1,0:T(8,128)(2,1)} %param.12), kind=kOutput, calls=%fused_computation.7 | convolution fusion | flops 1207959552 | bytes 6881280 | tf_op jit(solution)/shard_map/dot_general | solution.py:30
  120.6 5.1 %reshape.52 = bf16[128,3,2048]{2,1,0:T(4,128)(2,1)} reshape(bf16[384,2048]{1,0:T(8,128)(2,1)} %add_convert_fusion) | data formatting | bytes 3145728 | tf_op jit(solution)/shard_map/reshape | solution.py:89
  125.7 18.9 %all-to-all-done.1 = bf16[128,3,2048]{2,1,0:T(4,128)(2,1)} async-done(((bf16[128,3,2048]{2,1,0:T(4,128)(2,1)}), bf16[128,3,2048]{2,1,0:T(4,128)(2,1)}, u32[]{:S(2)}, u32[]{:S(2)}) %all-to-all-start.1) | async-done | bytes 1572896 | tf_op jit(solution)/shard_map/all_to_all | solution.py:77
  144.6 5.6 %all-to-all-start.3 = ((bf16[128,3,2048]{2,1,0:T(4,128)(2,1)}), bf16[128,3,2048]{2,1,0:T(4,128)(2,1)}, u32[]{:S(2)}, u32[]{:S(2)}) async-start(bf16[128,3,2048]{2,1,0:T(4,128)(2,1)} %reshape.52), calls=%async_computation.3 | async-start | bytes 4194304 | tf_op jit(solution)/shard_map/all_to_all | solution.py:88
  150.2 5.2 %fusion.12 = bf16[1,2048,768]{2,1,0:T(8,128)(2,1)} fusion(bf16[384,2048]{1,0:T(8,128)(2,1)} %reshape.47, bf16[384,768]{1,0:T(8,128)(2,1)} %get-tuple-element.6), kind=kOutput, calls=%fused_computation.16 | convolution fusion | flops 1209532416 | bytes 5308416 | tf_op jit(solution)/shard_map/dot_general | solution.py:34
  155.4 3.5 %fusion.13 = bf16[1,2048,768]{2,1,0:T(8,128)(2,1)} fusion(bf16[384,2048]{1,0:T(8,128)(2,1)S(1)} %copy-done.3, bf16[384,768]{1,0:T(8,128)(2,1)S(1)} %copy-done.8), kind=kOutput, calls=%fused_computation.17 | convolution fusion | flops 1209532416 | bytes 5308416 | tf_op jit(solution)/shard_map/dot_general | solution.py:37
  159.0 3.5 %fusion.14 = bf16[1,768,2048]{2,1,0:T(8,128)(2,1)} fusion(bf16[384,768]{1,0:T(8,128)(2,1)S(1)} %copy-done.10, bf16[384,2048]{1,0:T(8,128)(2,1)S(1)} %copy-done.1), kind=kOutput, calls=%fused_computation.18 | convolution fusion | flops 1209532416 | bytes 5308416 | tf_op jit(solution)/shard_map/dot_general | solution.py:40
  162.5 5.0 %reshape.49 = bf16[384,2048]{1,0:T(8,128)(2,1)} reshape(bf16[128,3,2048]{2,1,0:T(4,128)(2,1)} %all-to-all-done.1) | data formatting | bytes 3145728 | tf_op jit(solution)/shard_map/reshape | solution.py:98
  167.5 3.8 %fusion.22 = (f32[192]{0:T(256)}, bf16[192,2048]{1,0:T(8,128)(2,1)}) fusion(bf16[192,2048]{1,0:T(8,128)(2,1)} %param.10, f32[192]{0:T(256)S(1)} %copy-done.4, bf16[384,2048]{1,0:T(8,128)(2,1)} %reshape.49, s32[192]{0:T(256)S(1)} %convert_add_fusion), kind=kOutput, calls=%fused_computation.28 | convolution fusion | flops 304815936 | bytes 3148032 | tf_op jit(solution)/shard_map/dot_general | solution.py:96
  171.3 9.1 %all-to-all-done.3 = bf16[128,3,2048]{2,1,0:T(4,128)(2,1)} async-done(((bf16[128,3,2048]{2,1,0:T(4,128)(2,1)}), bf16[128,3,2048]{2,1,0:T(4,128)(2,1)}, u32[]{:S(2)}, u32[]{:S(2)}) %all-to-all-start.3) | async-done | bytes 1572896 | tf_op jit(solution)/shard_map/all_to_all | solution.py:88
  180.4 5.0 %reshape.53 = bf16[384,2048]{1,0:T(8,128)(2,1)} reshape(bf16[128,3,2048]{2,1,0:T(4,128)(2,1)} %all-to-all-done.3) | data formatting | bytes 3145728 | tf_op jit(solution)/shard_map/reshape | solution.py:104
  (29 shorter events, 16.5 us)
Async XLA Ops:
  0.6 96.7 %copy-start = (bf16[1,2048,768]{2,1,0:T(8,128)(2,1)S(1)}, bf16[1,2048,768]{2,1,0:T(8,128)(2,1)}, u32[]{:S(2)}) copy-start(bf16[1,2048,768]{2,1,0:T(8,128)(2,1)} %param.11) | copy-start | bytes 9437188
  10.6 42.0 %all-to-all-start.2 = ((bf16[128,3,2048]{2,1,0:T(4,128)(2,1)}), bf16[128,3,2048]{2,1,0:T(4,128)(2,1)}, u32[]{:S(2)}, u32[]{:S(2)}) async-start(bf16[128,3,2048]{2,1,0:T(4,128)(2,1)} %reshape.50), calls=%async_computation.2 | async-start | bytes 4194304 | tf_op jit(solution)/shard_map/all_to_all | solution.py:84
  52.6 35.8 %all-to-all-start = ((bf16[128,3,2048]{2,1,0:T(4,128)(2,1)}), bf16[128,3,2048]{2,1,0:T(4,128)(2,1)}, u32[]{:S(2)}, u32[]{:S(2)}) async-start(bf16[128,3,2048]{2,1,0:T(4,128)(2,1)} %reshape.46), calls=%async_computation | async-start | bytes 4194304 | tf_op jit(solution)/shard_map/all_to_all | solution.py:74
  93.4 3.9 %copy-start.2 = (bf16[384,2048]{1,0:T(8,128)(2,1)S(1)}, bf16[384,2048]{1,0:T(8,128)(2,1)}, u32[]{:S(2)}) copy-start(bf16[384,2048]{1,0:T(8,128)(2,1)} %reshape.47) | copy-start | bytes 4718596
  93.4 3.9 %copy-start.7 = (f32[384,768]{1,0:T(8,128)S(1)}, f32[384,768]{1,0:T(8,128)}, u32[]{:S(2)}) copy-start(f32[384,768]{1,0:T(8,128)} %fusion) | copy-start | bytes 3538948
  97.4 3.7 %copy-start.5 = (bf16[1,768,2048]{2,1,0:T(8,128)(2,1)S(1)}, bf16[1,768,2048]{2,1,0:T(8,128)(2,1)}, u32[]{:S(2)}) copy-start(bf16[1,768,2048]{2,1,0:T(8,128)(2,1)} %param.13) | copy-start | bytes 9437188
  100.2 0.9 copy-start.9
  108.8 35.8 %all-to-all-start.1 = ((bf16[128,3,2048]{2,1,0:T(4,128)(2,1)}), bf16[128,3,2048]{2,1,0:T(4,128)(2,1)}, u32[]{:S(2)}, u32[]{:S(2)}) async-start(bf16[128,3,2048]{2,1,0:T(4,128)(2,1)} %reshape.48), calls=%async_computation.1 | async-start | bytes 4194304 | tf_op jit(solution)/shard_map/all_to_all | solution.py:77
  114.4 3.6 %copy-start.6 = (bf16[384,768]{1,0:T(8,128)(2,1)S(1)}, bf16[384,768]{1,0:T(8,128)(2,1)}, u32[]{:S(2)}) copy-start(bf16[384,768]{1,0:T(8,128)(2,1)} %get-tuple-element.6) | copy-start | bytes 1769476
  144.6 35.8 %all-to-all-start.3 = ((bf16[128,3,2048]{2,1,0:T(4,128)(2,1)}), bf16[128,3,2048]{2,1,0:T(4,128)(2,1)}, u32[]{:S(2)}, u32[]{:S(2)}) async-start(bf16[128,3,2048]{2,1,0:T(4,128)(2,1)} %reshape.52), calls=%async_computation.3 | async-start | bytes 4194304 | tf_op jit(solution)/shard_map/all_to_all | solution.py:88
  150.2 5.2 %copy-start.3 = (bf16[384,2048]{1,0:T(8,128)(2,1)S(1)}, bf16[384,2048]{1,0:T(8,128)(2,1)}, u32[]{:S(2)}) copy-start(bf16[384,2048]{1,0:T(8,128)(2,1)} %reshape.47) | copy-start | bytes 4718596
  150.2 5.2 %copy-start.8 = (bf16[384,768]{1,0:T(8,128)(2,1)S(1)}, bf16[384,768]{1,0:T(8,128)(2,1)}, u32[]{:S(2)}) copy-start(bf16[384,768]{1,0:T(8,128)(2,1)} %get-tuple-element.7) | copy-start | bytes 1769476
  155.4 3.5 %copy-start.1 = (bf16[384,2048]{1,0:T(8,128)(2,1)S(1)}, bf16[384,2048]{1,0:T(8,128)(2,1)}, u32[]{:S(2)}) copy-start(bf16[384,2048]{1,0:T(8,128)(2,1)} %reshape.51) | copy-start | bytes 4718596
  155.4 3.5 %copy-start.10 = (bf16[384,768]{1,0:T(8,128)(2,1)S(1)}, bf16[384,768]{1,0:T(8,128)(2,1)}, u32[]{:S(2)}) copy-start(bf16[384,768]{1,0:T(8,128)(2,1)} %copy-done.9) | copy-start | bytes 1769476
  162.5 5.0 %copy-start.4 = (f32[192]{0:T(256)S(1)}, f32[192]{0:T(256)}, u32[]{:S(2)}) copy-start(f32[192]{0:T(256)} %param.9) | copy-start | bytes 2308
where the time goes:
time: 190 us; the launch traced here: 188 us
  waiting for transfers between devices  70.3 us (37%)
  matrix products  46 us (24%)
  local copies, waits for them, and re-layouts  41.7 us (22%)
  starting transfers between devices  28.8 us (15%)
    all_to_all x1, waiting for transfers between devices, local(): lax.all_to_all(send_grad, 'expert', split_axis=0, concat_axis=0, tiled=True)  22 us
    all_to_all x1, waiting for transfers between devices, local(): lax.all_to_all(send_rows, 'expert', split_axis=0, concat_axis=0, tiled=True)  20.3 us
    all_to_all x1, waiting for transfers between devices, local(): lax.all_to_all(expert_out.reshape(devices, capacity, width), 'expert', sp...  18.9 us
    all_to_all x1, starting transfers between devices, local(): lax.all_to_all(send_grad, 'expert', split_axis=0, concat_axis=0, tiled=True)  12 us
    all_to_all x1, waiting for transfers between devices, local(): lax.all_to_all(input_grad.reshape(devices, capacity, width), 'expert', sp...  9.06 us
    all_to_all x1, starting transfers between devices, local(): lax.all_to_all(expert_out.reshape(devices, capacity, width), 'expert', sp...  5.63 us
    all_to_all x1, starting transfers between devices, local(): lax.all_to_all(send_rows, 'expert', split_axis=0, concat_axis=0, tiled=True)  5.61 us
    all_to_all x1, starting transfers between devices, local(): lax.all_to_all(input_grad.reshape(devices, capacity, width), 'expert', sp...  5.61 us
  transfers between devices with their start and end apart: 4, of which 4 were waited for; matrix products, arithmetic and copies ran while one was open for 27% of the time, Pallas kernels for 0%

commit v1 on v0

v1 whole, which is shorter than its diff:
```python
import functools

import jax
import jax.numpy as jnp
from jax import lax
from jax.experimental import pallas as pl
from jax.experimental.pallas import tpu as pltpu
from jax.sharding import PartitionSpec as P

CAP = 3
MAIN = 1536
TAIL = 512
WIDTH = MAIN + TAIL
PACK = 8
GROUP = 32
SLAB = PACK * GROUP
NT = (((1,), (1,)), ((), ()))
TN = (((0,), (0,)), ((), ()))


def iota(shape, dim):
    return lax.broadcasted_iota(jnp.int32, shape, dim)


def column_of(row, count):
    wide = jnp.broadcast_to(row, (count, count))
    return jnp.sum(
        jnp.where(iota((count, count), 0) == iota((count, count), 1), wide, 0.0),
        axis=1,
        keepdims=True,
    )


def slot_codes(index_row, count):
    expert = column_of(index_row, count)
    same = expert == jnp.broadcast_to(index_row, (count, count))
    before = iota((count, count), 1) < iota((count, count), 0)
    rank = jnp.sum(jnp.where(same & before, 1.0, 0.0), axis=1, keepdims=True)
    return 4.0 * expert + rank


def dispatch_kernel(index_ref, weight_ref, rows_ref, cot_ref, out_ref, right, codes):
    count = rows_ref.shape[0]
    step = pl.program_id(0)

    @pl.when(step == 0)
    def _():
        code = slot_codes(index_ref[...].astype(jnp.float32), count)
        shape = (count, 4 * count)
        lane = iota(shape, 1)
        part = (
            (lane >= count).astype(jnp.int32)
            + (lane >= 2 * count).astype(jnp.int32)
            + (lane >= 3 * count).astype(jnp.int32)
        )
        placed = code + 1024.0 * part.astype(jnp.float32)
        picked = jnp.where(iota(shape, 0) == lane - count * part, placed, 0.0)
        codes[...] = jnp.broadcast_to(jnp.sum(picked, axis=0, keepdims=True), codes.shape)
        weight = column_of(weight_ref[...], count)
        grad = (weight * cot_ref[...].astype(jnp.float32)).astype(jnp.bfloat16)
        rows = rows_ref[...]
        right[0:count, :] = rows[:, :MAIN]
        right[count : 2 * count, :] = grad[:, :MAIN]
        for rank in range(CAP):
            block = slice(TAIL * rank, TAIL * (rank + 1))
            right[2 * count : 3 * count, block] = rows[:, MAIN:]
            right[3 * count :, block] = grad[:, MAIN:]

    row = iota((SLAB, 1), 0)
    place = row & (PACK - 1)
    target = (GROUP * step + (row >> 3)) * 4
    lanes = codes[0:1, :]
    for rank in range(CAP):
        wanted = jnp.where(
            place < 3,
            target + place,
            jnp.where(
                place < 6,
                target + place + (1024 - 3),
                jnp.where(place == 6, target + (2048 + rank), target + (3072 + rank)),
            ),
        ).astype(jnp.float32)
        left = jnp.where(wanted == lanes, 1.0, 0.0).astype(jnp.bfloat16)
        block = slice(TAIL * rank, TAIL * (rank + 1))
        out_ref[:, block] = jnp.dot(
            left, right[:, block], preferred_element_type=jnp.float32
        ).astype(jnp.bfloat16)


def dispatch(index, weight, rows, cot, devices):
    count = rows.shape[0]
    return pl.pallas_call(
        dispatch_kernel,
        grid=(devices // GROUP,),
        in_specs=[
            pl.BlockSpec((1, count), lambda i: (0, 0)),
            pl.BlockSpec((1, count), lambda i: (0, 0)),
            pl.BlockSpec((count, WIDTH), lambda i: (0, 0)),
            pl.BlockSpec((count, WIDTH), lambda i: (0, 0)),
        ],
        out_specs=pl.BlockSpec((SLAB, MAIN), lambda i: (i, 0)),
        out_shape=jax.ShapeDtypeStruct((devices * PACK, MAIN), jnp.bfloat16),
        scratch_shapes=[
            pltpu.VMEM((4 * count, MAIN), jnp.bfloat16),
            pltpu.VMEM((8, 4 * count), jnp.float32),
        ],
        compiler_params=pltpu.CompilerParams(vmem_limit_bytes=24 << 20),
        name="dispatch",
    )(index, weight, rows, cot)


def split_matrix():
    out, packed = iota((SLAB, SLAB), 0), iota((SLAB, SLAB), 1)
    return jnp.where(packed == (out & (GROUP - 1)) * PACK + (out >> 5), 1.0, 0.0).astype(
        jnp.bfloat16
    )


def join_matrix():
    packed, out = iota((SLAB, SLAB), 0), iota((SLAB, SLAB), 1)
    return jnp.where(packed == (out & (GROUP - 1)) * PACK + (out >> 5), 1.0, 0.0).astype(
        jnp.bfloat16
    )


def unpack(packed, matrix, first, second, group):
    span = CAP * GROUP
    base = span * group
    for rank in range(CAP):
        block = slice(TAIL * rank, TAIL * (rank + 1))
        part = jnp.dot(matrix, packed[:, block], preferred_element_type=jnp.float32).astype(
            jnp.bfloat16
        )
        first[base : base + span, block] = part[0:span]
        second[base : base + span, block] = part[span : 2 * span]
        low = base + GROUP * rank
        first[low : low + GROUP, MAIN:] = part[2 * span : 2 * span + GROUP]
        second[low : low + GROUP, MAIN:] = part[2 * span + GROUP :]


def expert_kernel(
    got,
    w_gate,
    w_up,
    w_down,
    send,
    rows_out,
    grad_out,
    hidden_out,
    gate_out,
    up_out,
    packed,
    rows,
    grad,
    hidden,
    gate_pre,
    up_pre,
    result,
    input_grad,
    stacked,
    in_sem,
    out_sem,
    send_sem,
):
    groups = got.shape[0] // SLAB
    span = CAP * GROUP

    def load(group):
        part = pl.ds(SLAB * group, SLAB)
        return pltpu.make_async_copy(got.at[part], packed.at[part], in_sem.at[group])

    for group in range(groups):
        load(group).start()
    matrix = split_matrix()
    for group in range(groups):
        load(group).wait()
        unpack(packed.at[SLAB * group : SLAB * (group + 1)], matrix, rows, grad, group)
    saves = [pltpu.make_async_copy(rows, rows_out, out_sem.at[0])]
    saves.append(pltpu.make_async_copy(grad, grad_out, out_sem.at[1]))
    for save in saves:
        save.start()

    x = rows[...]
    gate_act = jnp.dot(x, w_gate[...], preferred_element_type=jnp.float32)
    up_act = jnp.dot(x, w_up[...], preferred_element_type=jnp.float32)
    hidden_grad = lax.dot_general(grad[...], w_down[...], NT, preferred_element_type=jnp.float32)
    sigma = jax.nn.sigmoid(gate_act)
    silu_gate = gate_act * sigma
    hidden[...] = (silu_gate * up_act).astype(jnp.bfloat16)
    gate_pre[...] = (hidden_grad * up_act * sigma * (1.0 + gate_act * (1.0 - sigma))).astype(
        jnp.bfloat16
    )
    up_pre[...] = (hidden_grad * silu_gate).astype(jnp.bfloat16)
    for number, (part, target) in enumerate(
        ((hidden, hidden_out), (gate_pre, gate_out), (up_pre, up_out))
    ):
        save = pltpu.make_async_copy(part, target, out_sem.at[2 + number])
        save.start()
        saves.append(save)
    result[...] = jnp.dot(hidden[...], w_down[...], preferred_element_type=jnp.float32).astype(
        jnp.bfloat16
    )
    input_grad[...] = (
        lax.dot_general(gate_pre[...], w_gate[...], NT, preferred_element_type=jnp.float32)
        + lax.dot_general(up_pre[...], w_up[...], NT, preferred_element_type=jnp.float32)
    ).astype(jnp.bfloat16)

    matrix = join_matrix()
    for group in range(groups):
        base = span * group
        stacked[0:span, :] = result[base : base + span, :MAIN]
        stacked[span : 2 * span, :] = input_grad[base : base + span, :MAIN]
        for rank in range(CAP):
            block = slice(TAIL * rank, TAIL * (rank + 1))
            low = base + GROUP * rank
            stacked[2 * span : 2 * span + GROUP, block] = result[low : low + GROUP, MAIN:]
            stacked[2 * span + GROUP :, block] = input_grad[low : low + GROUP, MAIN:]
        packed[SLAB * group : SLAB * (group + 1), :] = jnp.dot(
            matrix, stacked[...], preferred_element_type=jnp.float32
        ).astype(jnp.bfloat16)
        part = pl.ds(SLAB * group, SLAB)
        save = pltpu.make_async_copy(packed.at[part], send.at[part], send_sem.at[group])
        save.start()
        saves.append(save)
    for save in saves:
        save.wait()


def expert(got, w_gate, w_up, w_down):
    slots = got.shape[0] // PACK * CAP
    units = w_gate.shape[1]
    anywhere = pl.BlockSpec(memory_space=pl.ANY)
    local = pl.BlockSpec(memory_space=pltpu.VMEM)
    wide = jax.ShapeDtypeStruct((slots, WIDTH), jnp.bfloat16)
    narrow = jax.ShapeDtypeStruct((slots, units), jnp.bfloat16)
    groups = got.shape[0] // SLAB
    return pl.pallas_call(
        expert_kernel,
        in_specs=[anywhere, local, local, local],
        out_specs=[anywhere] * 6,
        out_shape=[
            jax.ShapeDtypeStruct(got.shape, jnp.bfloat16),
            wide,
            wide,
            narrow,
            narrow,
            narrow,
        ],
        scratch_shapes=[
            pltpu.VMEM(got.shape, jnp.bfloat16),
            pltpu.VMEM((slots, WIDTH), jnp.bfloat16),
            pltpu.VMEM((slots, WIDTH), jnp.bfloat16),
            pltpu.VMEM((slots, units), jnp.bfloat16),
            pltpu.VMEM((slots, units), jnp.bfloat16),
            pltpu.VMEM((slots, units), jnp.bfloat16),
            pltpu.VMEM((slots, WIDTH), jnp.bfloat16),
            pltpu.VMEM((slots, WIDTH), jnp.bfloat16),
            pltpu.VMEM((SLAB, MAIN), jnp.bfloat16),
            pltpu.SemaphoreType.DMA((groups,)),
            pltpu.SemaphoreType.DMA((5,)),
            pltpu.SemaphoreType.DMA((groups,)),
        ],
        compiler_params=pltpu.CompilerParams(vmem_limit_bytes=48 << 20),
        cost_estimate=pl.CostEstimate(
            flops=12 * slots * WIDTH * units,
            bytes_accessed=4 * got.size + 6 * WIDTH * units + 4 * slots * WIDTH,
            transcendentals=slots * units,
        ),
        name="expert",
    )(got, w_gate, w_up, w_down)


def combine_kernel(
    index_ref, weight_ref, cot_ref, got_ref, out_ref, row_ref, wgrad_ref, first, second, matrix
):
    count = cot_ref.shape[0]
    step = pl.program_id(0)
    groups = pl.num_programs(0)
    span = CAP * GROUP

    @pl.when(step == 0)
    def _():
        matrix[...] = split_matrix()

    base = pl.multiple_of(span * step, span)
    for rank in range(CAP):
        block = slice(TAIL * rank, TAIL * (rank + 1))
        part = jnp.dot(
            matrix[...], got_ref[:, block], preferred_element_type=jnp.float32
        ).astype(jnp.bfloat16)
        first[pl.ds(base, span), block] = part[0:span]
        second[pl.ds(base, span), block] = part[span : 2 * span]
        low = pl.multiple_of(base + GROUP * rank, GROUP)
        first[pl.ds(low, GROUP), MAIN:] = part[2 * span : 2 * span + GROUP]
        second[pl.ds(low, GROUP), MAIN:] = part[2 * span + GROUP :]

    @pl.when(step == groups - 1)
    def _():
        slots = first.shape[0]
        code = slot_codes(index_ref[...].astype(jnp.float32), count)
        lane = iota((count, slots), 1)
        group = jnp.zeros_like(lane)
        for edge in range(1, slots // span):
            group = group + (lane >= span * edge).astype(jnp.int32)
        inner = lane - span * group
        rank = (inner >= GROUP).astype(jnp.int32) + (inner >= 2 * GROUP).astype(jnp.int32)
        device = GROUP * group + inner - GROUP * rank
        pick = jnp.where(code == (4 * device + rank).astype(jnp.float32), 1.0, 0.0).astype(
            jnp.bfloat16
        )
        weight = column_of(weight_ref[...], count)
        total = jnp.zeros((count, 1), jnp.float32)
        for low in range(0, WIDTH, TAIL):
            block = slice(low, low + TAIL)
            out = jnp.dot(pick, first[:, block], preferred_element_type=jnp.float32)
            out_ref[:, block] = (weight * out).astype(jnp.bfloat16)
            total += jnp.sum(
                cot_ref[:, block].astype(jnp.float32) * out, axis=1, keepdims=True
            )
            row_ref[:, block] = jnp.dot(
                pick, second[:, block], preferred_element_type=jnp.float32
            ).astype(jnp.bfloat16)
        eye = iota((count, count), 0) == iota((count, count), 1)
        wgrad_ref[...] = jnp.sum(jnp.where(eye, total, 0.0), axis=0, keepdims=True)


def combine(index, weight, cot, got):
    count = cot.shape[0]
    groups = got.shape[0] // SLAB
    slots = groups * CAP * GROUP
    whole = lambda i: (0, 0)
    return pl.pallas_call(
        combine_kernel,
        grid=(groups,),
        in_specs=[
            pl.BlockSpec((1, count), whole),
            pl.BlockSpec((1, count), whole),
            pl.BlockSpec((count, WIDTH), whole),
            pl.BlockSpec((SLAB, MAIN), lambda i: (i, 0)),
        ],
        out_specs=[
            pl.BlockSpec((count, WIDTH), whole),
            pl.BlockSpec((count, WIDTH), whole),
            pl.BlockSpec((1, count), whole),
        ],
        out_shape=[
            jax.ShapeDtypeStruct((count, WIDTH), jnp.bfloat16),
            jax.ShapeDtypeStruct((count, WIDTH), jnp.bfloat16),
            jax.ShapeDtypeStruct((1, count), jnp.float32),
        ],
        scratch_shapes=[
            pltpu.VMEM((slots, WIDTH), jnp.bfloat16),
            pltpu.VMEM((slots, WIDTH), jnp.bfloat16),
            pltpu.VMEM((SLAB, SLAB), jnp.bfloat16),
        ],
        compiler_params=pltpu.CompilerParams(vmem_limit_bytes=24 << 20),
        name="combine",
    )(index, weight, cot, got)


def exchange(packed, devices):
    moved = lax.all_to_all(
        packed.reshape(devices, PACK, MAIN), "expert", split_axis=0, concat_axis=0, tiled=True
    )
    return moved.reshape(packed.shape)


def weight_product(left, right):
    return lax.dot_general(left, right, TN, preferred_element_type=jnp.float32).astype(
        jnp.bfloat16
    )


def local(routed_rows, expert_index, route_weight, cotangent, gate_weight, up_weight, down_weight):
    devices = lax.axis_size("expert")
    count = routed_rows.shape[0]
    index = expert_index.reshape(1, count)
    weight = route_weight.reshape(1, count)
    packed = dispatch(index, weight, routed_rows, cotangent, devices)
    got = exchange(packed, devices)
    send, rows, grad, hidden, gate_pre, up_pre = expert(
        got, gate_weight[0], up_weight[0], down_weight[0]
    )
    back = exchange(send, devices)
    gate_grad = weight_product(rows, gate_pre)
    up_grad = weight_product(rows, up_pre)
    down_grad = weight_product(hidden, grad)
    layer_out, row_grad, weight_grad = combine(index, weight, cotangent, back)
    return (
        layer_out,
        row_grad,
        weight_grad.reshape(count),
        gate_grad[None],
        up_grad[None],
        down_grad[None],
    )


def solution(mesh):
    rows = P("expert", None)
    weights = P("expert", None, None)
    return jax.shard_map(
        local,
        mesh=mesh,
        in_specs=(rows, rows, P("expert"), rows, weights, weights, weights),
        out_specs=(rows, rows, P("expert"), weights, weights, weights),
        check_vma=False,
    )
```

time: 190 us -> 135 us (0.71)
  blocking collectives: 0 us -> 53.1 us
  waiting for transfers between devices: 70.3 us -> 29.5 us
  matrix products: 46 us -> 12.2 us
  local copies, waits for them, and re-layouts: 41.7 us -> 9.52 us
  Pallas kernels: 0 us -> 25 us
  starting transfers between devices: 28.8 us -> 4.57 us
    all_to_all x0 -> x1, blocking collectives: none -> 53.1 us  [exchange(): lax.all_to_all(packed.reshape(devices, PACK, MAIN), 'expert', split_axis=...]
    all_to_all x4 -> x1, waiting for transfers between devices: 70.3 us -> 29.5 us  [exchange(): lax.all_to_all(packed.reshape(devices, PACK, MAIN), 'expert', split_axis=...]
    reshape x8 -> x0, local copies, waits for them, and re-layouts: 40.8 us -> none  [the longest x1 5.15 us: local(): send_grad = send_grad.reshape(devices, capacity, width)]
    dot_general x14 -> x3, matrix products: 46 us -> 12.2 us  [weight_product(): lax.dot_general(left, right, TN, preferred_element_type=jnp.float32)]
    pallas_call x0 -> x3, Pallas kernels: none -> 25 us  [the longest x1 17.6 us: expert(): pl.pallas_call(expert_kernel, in_specs=[anywhere, local, local, local], o...]
    all_to_all x4 -> x1, starting transfers between devices: 28.8 us -> 4.57 us  [exchange(): lax.all_to_all(packed.reshape(devices, PACK, MAIN), 'expert', split_axis=...]
    unnamed x22 -> x32, local copies, waits for them, and re-layouts: 0.92 us -> 9.52 us
  transfers between devices with their start and end apart: 4 -> 1, of which waited for: 4 -> 1; matrix products, arithmetic and copies ran while one was open for 27% -> 9% of each run, Pallas kernels for 0% -> 0%
where the time goes in v1:
time: 135 us
  blocking collectives  53.1 us (39%)
  waiting for transfers between devices  29.5 us (22%)
  Pallas kernels  25 us (19%)
  matrix products  12.2 us (9%)
  local copies, waits for them, and re-layouts  9.52 us (7%)
  starting transfers between devices  4.57 us (3%)
    all_to_all x1, blocking collectives, exchange(): lax.all_to_all(packed.reshape(devices, PACK, MAIN), 'expert', split_axis=...  53.1 us
    all_to_all x1, waiting for transfers between devices, exchange(): lax.all_to_all(packed.reshape(devices, PACK, MAIN), 'expert', split_axis=...  29.5 us
    pallas_call x1, Pallas kernels, expert(): pl.pallas_call(expert_kernel, in_specs=[anywhere, local, local, local], o...  17.6 us
    dot_general x3, matrix products, weight_product(): lax.dot_general(left, right, TN, preferred_element_type=jnp.float32)  12.2 us
    unnamed x32, local copies, waits for them, and re-layouts  9.52 us
    all_to_all x1, starting transfers between devices, exchange(): lax.all_to_all(packed.reshape(devices, PACK, MAIN), 'expert', split_axis=...  4.57 us
    pallas_call x1, Pallas kernels, combine(): pl.pallas_call(combine_kernel, grid=(groups,), in_specs=[pl.BlockSpec((1,...  3.9 us
    pallas_call x1, Pallas kernels, dispatch(): pl.pallas_call(dispatch_kernel, grid=(devices // GROUP,), in_specs=[pl.Bl...  3.51 us
  transfers between devices with their start and end apart: 1, of which 1 were waited for; matrix products, arithmetic and copies ran while one was open for 9% of the time, Pallas kernels for 0%

profile of v1, /device:TPU:1, one launch (start us, length us, event | category | flops | bytes accessed | tf_op | source)
XLA Modules:
  0.0 134.6 jit_solution(11812025199540777186)
XLA Ops:
  0.6 0.0 copy-start
  0.6 1.1 copy-done
  1.8 1.1 copy-done.2
  2.9 0.7 copy-done.3
  3.6 0.7 copy-done.5
  4.3 3.5 %dispatch.1 = bf16[1024,1536]{1,0:T(8,128)(2,1)S(1)} custom-call(s32[1,192]{1,0:T(1,128)S(1)} %bitcast.24, f32[1,192]{1,0:T(1,128)S(1)} %bitcast.26, bf16[192,2048]{1,0:T(8,128)(2,1)S(1)} %copy-done.2, bf16[192,2048]{1,0:T(8,128)(2,1)S(1)} %copy-done), custom_call_target="tpu_custom_call" | custom-call | tf_op jit(solution)/shard_map/dispatch/pallas_call | solution.py:92
  7.8 53.1 %all_to_all.10 = bf16[128,8,1536]{2,1,0:T(8,128)(2,1)} all-to-all(bf16[128,8,1536]{2,1,0:T(8,128)(2,1)S(1)} %bitcast.23), channel_id=1, replica_groups=mesh['expert'=128] {'expert'}, dimensions={0} | all-to-all | bytes 6291456 | tf_op jit(solution)/shard_map/all_to_all | solution.py:362
  60.9 17.6 %expert.1 = (bf16[1024,1536]{1,0:T(8,128)(2,1)}, bf16[384,2048]{1,0:T(8,128)(2,1)S(1)}, bf16[384,2048]{1,0:T(8,128)(2,1)S(1)}, bf16[384,768]{1,0:T(8,128)(2,1)S(...) custom-call(bf16[1024,1536]{1,0:T(8,128)(2,1)} %bitcast.29, bf16[2048,768]{1,0:T(8,128)(2,1)} %bitcast.30, ...), custom_call_target="tpu_custom_call" | custom-call | flops 7247757312 | bytes 18874368 | tf_op jit(solution)/shard_map/expert/pallas_call | solution.py:237
  78.5 1.1 copy-done.7
  79.6 1.1 copy-done.9
  80.8 0.8 copy-done.11
  81.6 0.8 copy-done.13
  82.4 0.8 copy-done.15
  83.2 4.6 %all-to-all-start.1 = ((bf16[128,8,1536]{2,1,0:T(8,128)(2,1)}), bf16[128,8,1536]{2,1,0:T(8,128)(2,1)S(1)}, u32[]{:S(2)}, u32[]{:S(2)}) async-start(bf16[128,8,1536]{2,1,0:T(8,128)(2,1)} %bitcast.28), calls=%async_computation.1 | async-start | bytes 6291456 | tf_op jit(solution)/shard_map/all_to_all | solution.py:362
  87.8 0.0 copy-start.10
  87.8 0.0 copy-start.14
  87.8 5.2 %fusion = bf16[1,2048,768]{2,1,0:T(8,128)(2,1)} fusion(bf16[384,2048]{1,0:T(8,128)(2,1)} %copy-done.9, bf16[384,768]{1,0:T(8,128)(2,1)} %copy-done.15), kind=kOutput, calls=%fused_computation.3 | convolution fusion | flops 1209532416 | bytes 5308416 | tf_op jit(solution)/shard_map/dot_general | solution.py:369
  93.0 0.0 copy-done.10
  93.0 0.0 copy-start.12
  93.0 3.5 %fusion.1 = bf16[1,2048,768]{2,1,0:T(8,128)(2,1)} fusion(bf16[384,2048]{1,0:T(8,128)(2,1)S(1)} %copy-done.10, bf16[384,768]{1,0:T(8,128)(2,1)S(1)} %copy-done.14), kind=kOutput, calls=%fused_computation.4 | convolution fusion | flops 1209532416 | bytes 5308416 | tf_op jit(solution)/shard_map/dot_general | solution.py:369
  96.5 3.5 %fusion.2 = bf16[1,768,2048]{2,1,0:T(8,128)(2,1)} fusion(bf16[384,768]{1,0:T(8,128)(2,1)S(1)} %copy-done.12, bf16[384,2048]{1,0:T(8,128)(2,1)S(1)} %copy-done.8), kind=kOutput, calls=%fused_computation.5 | convolution fusion | flops 1209532416 | bytes 5308416 | tf_op jit(solution)/shard_map/dot_general | solution.py:369
  100.0 29.5 %all-to-all-done.1 = bf16[128,8,1536]{2,1,0:T(8,128)(2,1)S(1)} async-done(((bf16[128,8,1536]{2,1,0:T(8,128)(2,1)}), bf16[128,8,1536]{2,1,0:T(8,128)(2,1)S(1)}, u32[]{:S(2)}, u32[]{:S(2)}) %all-to-all-start.1) | async-done | bytes 3145760 | tf_op jit(solution)/shard_map/all_to_all | solution.py:362
  129.6 1.1 copy-done.1
  130.7 3.9 %combine.1 = (bf16[192,2048]{1,0:T(8,128)(2,1)}, bf16[192,2048]{1,0:T(8,128)(2,1)}, f32[1,192]{1,0:T(1,128)}) custom-call(s32[1,192]{1,0:T(1,128)S(1)} %bitcast.25, f32[1,192]{1,0:T(1,128)S(1)} %bitcast.27, bf16[192,2048]{1,0:T(8,128)(2,1)S(1)} %copy-done.1, bf16[1024,1536]{1,0:T(8,128)(2,1)S(1)} %bitcast.22), custom_call_target="tpu_custom_call" | custom-call | tf_op jit(solution)/shard_map/combine/pallas_call | solution.py:332
  (17 shorter events, 0.0 us)
Async XLA Ops:
  0.6 1.1 copy-start
  1.8 1.1 copy-start.2
  2.9 0.7 copy-start.3
  3.6 0.7 copy-start.5
  78.4 1.2 copy-start.7
  79.6 1.1 copy-start.9
  80.8 0.8 copy-start.11
  81.6 0.8 copy-start.13
  82.4 0.8 copy-start.15
  83.2 46.4 %all-to-all-start.1 = ((bf16[128,8,1536]{2,1,0:T(8,128)(2,1)}), bf16[128,8,1536]{2,1,0:T(8,128)(2,1)S(1)}, u32[]{:S(2)}, u32[]{:S(2)}) async-start(bf16[128,8,1536]{2,1,0:T(8,128)(2,1)} %bitcast.28), calls=%async_computation.1 | async-start | bytes 6291456 | tf_op jit(solution)/shard_map/all_to_all | solution.py:362
  87.8 5.2 %copy-start.10 = (bf16[384,2048]{1,0:T(8,128)(2,1)S(1)}, bf16[384,2048]{1,0:T(8,128)(2,1)}, u32[]{:S(2)}) copy-start(bf16[384,2048]{1,0:T(8,128)(2,1)} %copy-done.9) | copy-start | bytes 4718596
  87.8 5.2 %copy-start.14 = (bf16[384,768]{1,0:T(8,128)(2,1)S(1)}, bf16[384,768]{1,0:T(8,128)(2,1)}, u32[]{:S(2)}) copy-start(bf16[384,768]{1,0:T(8,128)(2,1)} %copy-done.13) | copy-start | bytes 1769476
  93.0 3.5 %copy-start.8 = (bf16[384,2048]{1,0:T(8,128)(2,1)S(1)}, bf16[384,2048]{1,0:T(8,128)(2,1)}, u32[]{:S(2)}) copy-start(bf16[384,2048]{1,0:T(8,128)(2,1)} %copy-done.7) | copy-start | bytes 4718596
  93.0 3.5 %copy-start.12 = (bf16[384,768]{1,0:T(8,128)(2,1)S(1)}, bf16[384,768]{1,0:T(8,128)(2,1)}, u32[]{:S(2)}) copy-start(bf16[384,768]{1,0:T(8,128)(2,1)} %copy-done.11) | copy-start | bytes 1769476
  96.5 33.1 %copy-start.4 = (s32[192,1]{0,1:T(1,128)S(1)}, s32[192,1]{0,1:T(1,128)}, u32[]{:S(2)}) copy-start(s32[192,1]{0,1:T(1,128)} %param.8) | copy-start | bytes 2308
  96.5 33.1 %copy-start.6 = (f32[192]{0:T(256)S(1)}, f32[192]{0:T(256)}, u32[]{:S(2)}) copy-start(f32[192]{0:T(256)} %param.9) | copy-start | bytes 2308
  129.6 1.1 copy-start.1

commit v2 on v1

v2 whole, which is shorter than its diff:
```python
import functools

import jax
import jax.numpy as jnp
from jax import lax
from jax.experimental import pallas as pl
from jax.experimental.pallas import tpu as pltpu
from jax.sharding import PartitionSpec as P

CAP = 3
MAIN = 1536
TAIL = 512
WIDTH = MAIN + TAIL
PACK = 8
GROUP = 32
SLAB = PACK * GROUP
NT = (((1,), (1,)), ((), ()))
TN = (((0,), (0,)), ((), ()))


def iota(shape, dim):
    return lax.broadcasted_iota(jnp.int32, shape, dim)


def column_of(row, count):
    wide = jnp.broadcast_to(row, (count, count))
    return jnp.sum(
        jnp.where(iota((count, count), 0) == iota((count, count), 1), wide, 0.0),
        axis=1,
        keepdims=True,
    )


def slot_codes(index_row, count):
    expert = column_of(index_row, count)
    same = expert == jnp.broadcast_to(index_row, (count, count))
    before = iota((count, count), 1) < iota((count, count), 0)
    rank = jnp.sum(jnp.where(same & before, 1.0, 0.0), axis=1, keepdims=True)
    return 4.0 * expert + rank


def dispatch_kernel(
    index_hbm, weight_hbm, rows_hbm, cot_hbm, out_ref, index, weight, rows, cot, right, in_sem
):
    count = rows.shape[0]
    loads = [
        pltpu.make_async_copy(source, target, in_sem.at[number])
        for number, (source, target) in enumerate(
            ((index_hbm, index), (weight_hbm, weight), (rows_hbm, rows), (cot_hbm, cot))
        )
    ]
    for load in loads:
        load.start()
    loads[0].wait()
    code = slot_codes(index[...].astype(jnp.float32), count)
    shape = (count, 4 * count)
    lane = iota(shape, 1)
    part = (
        (lane >= count).astype(jnp.int32)
        + (lane >= 2 * count).astype(jnp.int32)
        + (lane >= 3 * count).astype(jnp.int32)
    )
    placed = code + 1024.0 * part.astype(jnp.float32)
    picked = jnp.where(iota(shape, 0) == lane - count * part, placed, 0.0)
    lanes = jnp.sum(picked, axis=0, keepdims=True)
    loads[1].wait()
    scale = column_of(weight[...], count)
    loads[2].wait()
    right[0:count, :] = rows[:, :MAIN]
    for rank in range(CAP):
        right[2 * count : 3 * count, TAIL * rank : TAIL * (rank + 1)] = rows[:, MAIN:]
    loads[3].wait()
    grad = (scale * cot[...].astype(jnp.float32)).astype(jnp.bfloat16)
    right[count : 2 * count, :] = grad[:, :MAIN]
    for rank in range(CAP):
        right[3 * count :, TAIL * rank : TAIL * (rank + 1)] = grad[:, MAIN:]

    row = iota((SLAB, 1), 0)
    place = row & (PACK - 1)
    for group in range(out_ref.shape[0] // SLAB):
        target = (GROUP * group + (row >> 3)) * 4
        for rank in range(CAP):
            wanted = jnp.where(
                place < 3,
                target + place,
                jnp.where(
                    place < 6,
                    target + place + (1024 - 3),
                    jnp.where(place == 6, target + (2048 + rank), target + (3072 + rank)),
                ),
            ).astype(jnp.float32)
            left = jnp.where(wanted == lanes, 1.0, 0.0).astype(jnp.bfloat16)
            block = slice(TAIL * rank, TAIL * (rank + 1))
            out_ref[SLAB * group : SLAB * (group + 1), block] = jnp.dot(
                left, right[:, block], preferred_element_type=jnp.float32
            ).astype(jnp.bfloat16)


def in_hbm(array):
    return pltpu.with_memory_space_constraint(array, pltpu.HBM)


def in_vmem(array):
    return pltpu.with_memory_space_constraint(array, pltpu.VMEM)


ANYWHERE = pl.BlockSpec(memory_space=pl.ANY)
LOCAL = pl.BlockSpec(memory_space=pltpu.VMEM)


def dispatch(index, weight, rows, cot, devices):
    count = rows.shape[0]
    return pl.pallas_call(
        dispatch_kernel,
        in_specs=[ANYWHERE] * 4,
        out_specs=LOCAL,
        out_shape=pltpu.VMEM((devices * PACK, MAIN), jnp.bfloat16),
        scratch_shapes=[
            pltpu.VMEM((1, count), jnp.int32),
            pltpu.VMEM((1, count), jnp.float32),
            pltpu.VMEM((count, WIDTH), jnp.bfloat16),
            pltpu.VMEM((count, WIDTH), jnp.bfloat16),
            pltpu.VMEM((4 * count, MAIN), jnp.bfloat16),
            pltpu.SemaphoreType.DMA((4,)),
        ],
        compiler_params=pltpu.CompilerParams(vmem_limit_bytes=24 << 20),
        name="dispatch",
    )(in_hbm(index), in_hbm(weight), in_hbm(rows), in_hbm(cot))


def split_matrix():
    out, packed = iota((SLAB, SLAB), 0), iota((SLAB, SLAB), 1)
    return jnp.where(packed == (out & (GROUP - 1)) * PACK + (out >> 5), 1.0, 0.0).astype(
        jnp.bfloat16
    )


def join_matrix():
    packed, out = iota((SLAB, SLAB), 0), iota((SLAB, SLAB), 1)
    return jnp.where(packed == (out & (GROUP - 1)) * PACK + (out >> 5), 1.0, 0.0).astype(
        jnp.bfloat16
    )


def unpack(packed, matrix, first, second, group):
    span = CAP * GROUP
    base = span * group
    for rank in range(CAP):
        block = slice(TAIL * rank, TAIL * (rank + 1))
        part = jnp.dot(matrix, packed[:, block], preferred_element_type=jnp.float32).astype(
            jnp.bfloat16
        )
        first[base : base + span, block] = part[0:span]
        second[base : base + span, block] = part[span : 2 * span]
        low = base + GROUP * rank
        first[low : low + GROUP, MAIN:] = part[2 * span : 2 * span + GROUP]
        second[low : low + GROUP, MAIN:] = part[2 * span + GROUP :]


def expert_kernel(
    got,
    w_gate,
    w_up,
    w_down,
    send,
    rows_out,
    grad_out,
    hidden_out,
    gate_out,
    up_out,
    packed,
    rows,
    grad,
    hidden,
    gate_pre,
    up_pre,
    result,
    input_grad,
    stacked,
    out_sem,
    send_sem,
):
    groups = got.shape[0] // SLAB
    span = CAP * GROUP

    matrix = split_matrix()
    for group in range(groups):
        unpack(got.at[SLAB * group : SLAB * (group + 1)], matrix, rows, grad, group)
    saves = [pltpu.make_async_copy(rows, rows_out, out_sem.at[0])]
    saves.append(pltpu.make_async_copy(grad, grad_out, out_sem.at[1]))
    for save in saves:
        save.start()

    x = rows[...]
    gate_act = jnp.dot(x, w_gate[...], preferred_element_type=jnp.float32)
    up_act = jnp.dot(x, w_up[...], preferred_element_type=jnp.float32)
    hidden_grad = lax.dot_general(grad[...], w_down[...], NT, preferred_element_type=jnp.float32)
    sigma = jax.nn.sigmoid(gate_act)
    silu_gate = gate_act * sigma
    hidden[...] = (silu_gate * up_act).astype(jnp.bfloat16)
    gate_pre[...] = (hidden_grad * up_act * sigma * (1.0 + gate_act * (1.0 - sigma))).astype(
        jnp.bfloat16
    )
    up_pre[...] = (hidden_grad * silu_gate).astype(jnp.bfloat16)
    for number, (part, target) in enumerate(
        ((hidden, hidden_out), (gate_pre, gate_out), (up_pre, up_out))
    ):
        save = pltpu.make_async_copy(part, target, out_sem.at[2 + number])
        save.start()
        saves.append(save)
    result[...] = jnp.dot(hidden[...], w_down[...], preferred_element_type=jnp.float32).astype(
        jnp.bfloat16
    )
    input_grad[...] = (
        lax.dot_general(gate_pre[...], w_gate[...], NT, preferred_element_type=jnp.float32)
        + lax.dot_general(up_pre[...], w_up[...], NT, preferred_element_type=jnp.float32)
    ).astype(jnp.bfloat16)

    matrix = join_matrix()
    for group in range(groups):
        base = span * group
        stacked[0:span, :] = result[base : base + span, :MAIN]
        stacked[span : 2 * span, :] = input_grad[base : base + span, :MAIN]
        for rank in range(CAP):
            block = slice(TAIL * rank, TAIL * (rank + 1))
            low = base + GROUP * rank
            stacked[2 * span : 2 * span + GROUP, block] = result[low : low + GROUP, MAIN:]
            stacked[2 * span + GROUP :, block] = input_grad[low : low + GROUP, MAIN:]
        packed[SLAB * group : SLAB * (group + 1), :] = jnp.dot(
            matrix, stacked[...], preferred_element_type=jnp.float32
        ).astype(jnp.bfloat16)
        part = pl.ds(SLAB * group, SLAB)
        save = pltpu.make_async_copy(packed.at[part], send.at[part], send_sem.at[group])
        save.start()
        saves.append(save)
    for save in saves:
        save.wait()


def expert(got, w_gate, w_up, w_down):
    slots = got.shape[0] // PACK * CAP
    units = w_gate.shape[1]
    wide = pltpu.HBM((slots, WIDTH), jnp.bfloat16)
    narrow = pltpu.HBM((slots, units), jnp.bfloat16)
    groups = got.shape[0] // SLAB
    return pl.pallas_call(
        expert_kernel,
        in_specs=[LOCAL] * 4,
        out_specs=[ANYWHERE] * 6,
        out_shape=[
            pltpu.HBM(got.shape, jnp.bfloat16),
            wide,
            wide,
            narrow,
            narrow,
            narrow,
        ],
        scratch_shapes=[
            pltpu.VMEM(got.shape, jnp.bfloat16),
            pltpu.VMEM((slots, WIDTH), jnp.bfloat16),
            pltpu.VMEM((slots, WIDTH), jnp.bfloat16),
            pltpu.VMEM((slots, units), jnp.bfloat16),
            pltpu.VMEM((slots, units), jnp.bfloat16),
            pltpu.VMEM((slots, units), jnp.bfloat16),
            pltpu.VMEM((slots, WIDTH), jnp.bfloat16),
            pltpu.VMEM((slots, WIDTH), jnp.bfloat16),
            pltpu.VMEM((SLAB, MAIN), jnp.bfloat16),
            pltpu.SemaphoreType.DMA((5,)),
            pltpu.SemaphoreType.DMA((groups,)),
        ],
        compiler_params=pltpu.CompilerParams(vmem_limit_bytes=48 << 20),
        cost_estimate=pl.CostEstimate(
            flops=12 * slots * WIDTH * units,
            bytes_accessed=4 * got.size + 6 * WIDTH * units + 4 * slots * WIDTH,
            transcendentals=slots * units,
        ),
        name="expert",
    )(in_vmem(got), in_vmem(w_gate), in_vmem(w_up), in_vmem(w_down))


def combine_kernel(
    index_hbm,
    weight_hbm,
    cot_hbm,
    got,
    out_hbm,
    row_hbm,
    wgrad_ref,
    index,
    weight,
    cot,
    first,
    second,
    out,
    row,
    in_sem,
    out_sem,
):
    count = cot.shape[0]
    slots = first.shape[0]
    span = CAP * GROUP
    loads = [
        pltpu.make_async_copy(source, target, in_sem.at[number])
        for number, (source, target) in enumerate(
            ((index_hbm, index), (weight_hbm, weight), (cot_hbm, cot))
        )
    ]
    for load in loads:
        load.start()
    matrix = split_matrix()
    for group in range(got.shape[0] // SLAB):
        unpack(got.at[SLAB * group : SLAB * (group + 1)], matrix, first, second, group)
    loads[0].wait()
    code = slot_codes(index[...].astype(jnp.float32), count)
    lane = iota((count, slots), 1)
    group = jnp.zeros_like(lane)
    for edge in range(1, slots // span):
        group = group + (lane >= span * edge).astype(jnp.int32)
    inner = lane - span * group
    rank = (inner >= GROUP).astype(jnp.int32) + (inner >= 2 * GROUP).astype(jnp.int32)
    device = GROUP * group + inner - GROUP * rank
    pick = jnp.where(code == (4 * device + rank).astype(jnp.float32), 1.0, 0.0).astype(
        jnp.bfloat16
    )
    loads[1].wait()
    scale = column_of(weight[...], count)
    loads[2].wait()
    total = jnp.zeros((count, 1), jnp.float32)
    saves = []

    def save(source, target):
        copy = pltpu.make_async_copy(source, target, out_sem.at[len(saves)])
        copy.start()
        saves.append(copy)

    for low in range(0, WIDTH, TAIL):
        block = slice(low, low + TAIL)
        value = jnp.dot(pick, first[:, block], preferred_element_type=jnp.float32)
        out[:, block] = (scale * value).astype(jnp.bfloat16)
        save(out.at[:, block], out_hbm.at[:, block])
        total += jnp.sum(cot[:, block].astype(jnp.float32) * value, axis=1, keepdims=True)
        row[:, block] = jnp.dot(
            pick, second[:, block], preferred_element_type=jnp.float32
        ).astype(jnp.bfloat16)
        save(row.at[:, block], row_hbm.at[:, block])
    eye = iota((count, count), 0) == iota((count, count), 1)
    wgrad_ref[...] = jnp.sum(jnp.where(eye, total, 0.0), axis=0, keepdims=True)
    for copy in saves:
        copy.wait()


def combine(index, weight, cot, got):
    count = cot.shape[0]
    slots = got.shape[0] // PACK * CAP
    return pl.pallas_call(
        combine_kernel,
        in_specs=[ANYWHERE, ANYWHERE, ANYWHERE, LOCAL],
        out_specs=[ANYWHERE, ANYWHERE, LOCAL],
        out_shape=[
            pltpu.HBM((count, WIDTH), jnp.bfloat16),
            pltpu.HBM((count, WIDTH), jnp.bfloat16),
            jax.ShapeDtypeStruct((1, count), jnp.float32),
        ],
        scratch_shapes=[
            pltpu.VMEM((1, count), jnp.int32),
            pltpu.VMEM((1, count), jnp.float32),
            pltpu.VMEM((count, WIDTH), jnp.bfloat16),
            pltpu.VMEM((slots, WIDTH), jnp.bfloat16),
            pltpu.VMEM((slots, WIDTH), jnp.bfloat16),
            pltpu.VMEM((count, WIDTH), jnp.bfloat16),
            pltpu.VMEM((count, WIDTH), jnp.bfloat16),
            pltpu.SemaphoreType.DMA((3,)),
            pltpu.SemaphoreType.DMA((2 * WIDTH // TAIL,)),
        ],
        compiler_params=pltpu.CompilerParams(vmem_limit_bytes=24 << 20),
        name="combine",
    )(in_hbm(index), in_hbm(weight), in_hbm(cot), in_vmem(got))


def exchange(packed, devices):
    moved = lax.all_to_all(
        packed.reshape(devices, PACK, MAIN), "expert", split_axis=0, concat_axis=0, tiled=True
    )
    return moved.reshape(packed.shape)


def weight_product(left, right):
    return lax.dot_general(left, right, TN, preferred_element_type=jnp.float32).astype(
        jnp.bfloat16
    )


def local(routed_rows, expert_index, route_weight, cotangent, gate_weight, up_weight, down_weight):
    devices = lax.axis_size("expert")
    count = routed_rows.shape[0]
    index = expert_index.reshape(1, count)
    weight = route_weight.reshape(1, count)
    packed = dispatch(index, weight, routed_rows, cotangent, devices)
    got = exchange(packed, devices)
    send, rows, grad, hidden, gate_pre, up_pre = expert(
        got, gate_weight[0], up_weight[0], down_weight[0]
    )
    back = exchange(send, devices)
    gate_grad = weight_product(rows, gate_pre)
    up_grad = weight_product(rows, up_pre)
    down_grad = weight_product(hidden, grad)
    layer_out, row_grad, weight_grad = combine(index, weight, cotangent, back)
    return (
        layer_out,
        row_grad,
        weight_grad.reshape(count),
        gate_grad[None],
        up_grad[None],
        down_grad[None],
    )


def solution(mesh):
    rows = P("expert", None)
    weights = P("expert", None, None)
    return jax.shard_map(
        local,
        mesh=mesh,
        in_specs=(rows, rows, P("expert"), rows, weights, weights, weights),
        out_specs=(rows, rows, P("expert"), weights, weights, weights),
        check_vma=False,
    )
```

time: 135 us -> 120 us (0.89)
  local copies, waits for them, and re-layouts: 9.52 us -> 0.04 us
  Pallas kernels: 25 us -> 19 us
    unnamed x32 -> x14, local copies, waits for them, and re-layouts: 9.52 us -> 0.04 us
    pallas_call x3, Pallas kernels: 25 us -> 19 us  [the longest x1 10.5 us: expert(): pl.pallas_call(expert_kernel, in_specs=[LOCAL] * 4, out_specs=[ANYWHERE]...]
  transfers between devices with their start and end apart: 1 -> 1, of which waited for: 1 -> 1; matrix products, arithmetic and copies ran while one was open for 9% -> 10% of each run, Pallas kernels for 0% -> 0%
where the time goes in v2:
time: 120 us; the launch traced here: 119 us
  blocking collectives  53 us (44%)
  waiting for transfers between devices  29.6 us (25%)
  Pallas kernels  19 us (16%)
  matrix products  12.2 us (10%)
  starting transfers between devices  4.76 us (4%)
    all_to_all x1, blocking collectives, exchange(): lax.all_to_all(packed.reshape(devices, PACK, MAIN), 'expert', split_axis=...  53 us
    all_to_all x1, waiting for transfers between devices, exchange(): lax.all_to_all(packed.reshape(devices, PACK, MAIN), 'expert', split_axis=...  29.6 us
    dot_general x3, matrix products, weight_product(): lax.dot_general(left, right, TN, preferred_element_type=jnp.float32)  12.2 us
    pallas_call x1, Pallas kernels, expert(): pl.pallas_call(expert_kernel, in_specs=[LOCAL] * 4, out_specs=[ANYWHERE]...  10.5 us
    all_to_all x1, starting transfers between devices, exchange(): lax.all_to_all(packed.reshape(devices, PACK, MAIN), 'expert', split_axis=...  4.76 us
    pallas_call x1, Pallas kernels, combine(): pl.pallas_call(combine_kernel, in_specs=[ANYWHERE, ANYWHERE, ANYWHERE, LO...  4.28 us
    pallas_call x1, Pallas kernels, dispatch(): pl.pallas_call(dispatch_kernel, in_specs=[ANYWHERE] * 4, out_specs=LOCAL,...  4.23 us
  transfers between devices with their start and end apart: 1, of which 1 were waited for; matrix products, arithmetic and copies ran while one was open for 10% of the time, Pallas kernels for 0%

profile of v2, /device:TPU:1, one launch (start us, length us, event | category | flops | bytes accessed | tf_op | source)
XLA Modules:
  0.0 119.5 jit_solution(15853568081526273663)
XLA Ops:
  0.6 0.0 copy-start.2
  0.6 4.2 %dispatch.1 = bf16[1024,1536]{1,0:T(8,128)(2,1)S(1)} custom-call(s32[1,192]{1,0:T(1,128)} %bitcast.29, f32[1,192]{1,0:T(1,128)} %bitcast.31, bf16[192,2048]{1,0:T(8,128)(2,1)} %rows_hbm.1, bf16[192,2048]{1,0:T(8,128)(2,1)} %cot_hbm.3), custom_call_target="tpu_custom_call" | custom-call | tf_op jit(solution)/shard_map/dispatch/pallas_call | solution.py:113
  4.9 0.0 copy-start
  4.9 0.0 copy-start.1
  4.9 53.0 %all_to_all.10 = bf16[128,8,1536]{2,1,0:T(8,128)(2,1)S(1)} all-to-all(bf16[128,8,1536]{2,1,0:T(8,128)(2,1)S(1)} %bitcast.23), channel_id=1, replica_groups=mesh['expert'=128] {'expert'}, dimensions={0} | all-to-all | bytes 6291456 | tf_op jit(solution)/shard_map/all_to_all | solution.py:381
  57.9 0.0 copy-done.2
  57.9 0.0 copy-done
  57.9 0.0 copy-done.1
  57.9 10.5 %expert.1 = (bf16[1024,1536]{1,0:T(8,128)(2,1)}, bf16[384,2048]{1,0:T(8,128)(2,1)}, bf16[384,2048]{1,0:T(8,128)(2,1)}, bf16[384,768]{1,0:T(8,128)(2,1)}, bf16[38...) custom-call(bf16[1024,1536]{1,0:T(8,128)(2,1)S(1)} %bitcast.24, bf16[2048,768]{1,0:T(8,128)(2,1)S(1)} %bitcast.25, ...), custom_call_target="tpu_custom_call" | custom-call | flops 7247757312 | bytes 18874368 | tf_op jit(solution)/shard_map/expert/pallas_call | solution.py:246
  68.4 4.8 %all-to-all-start.1 = ((bf16[128,8,1536]{2,1,0:T(8,128)(2,1)}), bf16[128,8,1536]{2,1,0:T(8,128)(2,1)S(1)}, u32[]{:S(2)}, u32[]{:S(2)}) async-start(bf16[128,8,1536]{2,1,0:T(8,128)(2,1)} %bitcast.28), calls=%async_computation.1 | async-start | bytes 6291456 | tf_op jit(solution)/shard_map/all_to_all | solution.py:381
  73.2 0.0 copy-start.4
  73.2 0.0 copy-start.6
  73.2 5.2 %fusion = bf16[1,2048,768]{2,1,0:T(8,128)(2,1)} fusion(bf16[384,2048]{1,0:T(8,128)(2,1)} %get-tuple-element.19, bf16[384,768]{1,0:T(8,128)(2,1)} %get-tuple-element.20), kind=kOutput, calls=%fused_computation.3 | convolution fusion | flops 1209532416 | bytes 5308416 | tf_op jit(solution)/shard_map/dot_general | solution.py:388
  78.4 0.0 copy-done.4
  78.4 0.0 copy-done.6
  78.4 0.0 copy-start.3
  78.4 0.0 copy-start.5
  78.4 3.5 %fusion.1 = bf16[1,2048,768]{2,1,0:T(8,128)(2,1)} fusion(bf16[384,2048]{1,0:T(8,128)(2,1)S(1)} %copy-done.4, bf16[384,768]{1,0:T(8,128)(2,1)S(1)} %copy-done.6), kind=kOutput, calls=%fused_computation.4 | convolution fusion | flops 1209532416 | bytes 5308416 | tf_op jit(solution)/shard_map/dot_general | solution.py:388
  81.9 0.0 copy-done.3
  81.9 0.0 copy-done.5
  82.0 3.5 %fusion.2 = bf16[1,768,2048]{2,1,0:T(8,128)(2,1)} fusion(bf16[384,768]{1,0:T(8,128)(2,1)S(1)} %copy-done.5, bf16[384,2048]{1,0:T(8,128)(2,1)S(1)} %copy-done.3), kind=kOutput, calls=%fused_computation.5 | convolution fusion | flops 1209532416 | bytes 5308416 | tf_op jit(solution)/shard_map/dot_general | solution.py:388
  85.5 29.6 %all-to-all-done.1 = bf16[128,8,1536]{2,1,0:T(8,128)(2,1)S(1)} async-done(((bf16[128,8,1536]{2,1,0:T(8,128)(2,1)}), bf16[128,8,1536]{2,1,0:T(8,128)(2,1)S(1)}, u32[]{:S(2)}, u32[]{:S(2)}) %all-to-all-start.1) | async-done | bytes 3145760 | tf_op jit(solution)/shard_map/all_to_all | solution.py:381
  115.0 4.3 %combine.1 = (bf16[192,2048]{1,0:T(8,128)(2,1)}, bf16[192,2048]{1,0:T(8,128)(2,1)}, f32[1,192]{1,0:T(1,128)}) custom-call(s32[1,192]{1,0:T(1,128)} %bitcast.30, f32[1,192]{1,0:T(1,128)} %bitcast.32, bf16[192,2048]{1,0:T(8,128)(2,1)} %cot_hbm.3, bf16[1024,1536]{1,0:T(8,128)(2,1)S(1)} %bitcast.22), custom_call_target="tpu_custom_call" | custom-call | tf_op jit(solution)/shard_map/combine/pallas_call | solution.py:355
Async XLA Ops:
  0.6 57.3 %copy-start.2 = (bf16[1,768,2048]{2,1,0:T(8,128)(2,1)S(1)}, bf16[1,768,2048]{2,1,0:T(8,128)(2,1)}, u32[]{:S(2)}) copy-start(bf16[1,768,2048]{2,1,0:T(8,128)(2,1)} %param.13) | copy-start | bytes 9437188
  4.9 53.0 %copy-start = (bf16[1,2048,768]{2,1,0:T(8,128)(2,1)S(1)}, bf16[1,2048,768]{2,1,0:T(8,128)(2,1)}, u32[]{:S(2)}) copy-start(bf16[1,2048,768]{2,1,0:T(8,128)(2,1)} %param.11) | copy-start | bytes 9437188
  4.9 53.0 %copy-start.1 = (bf16[1,2048,768]{2,1,0:T(8,128)(2,1)S(1)}, bf16[1,2048,768]{2,1,0:T(8,128)(2,1)}, u32[]{:S(2)}) copy-start(bf16[1,2048,768]{2,1,0:T(8,128)(2,1)} %param.12) | copy-start | bytes 9437188
  68.4 46.6 %all-to-all-start.1 = ((bf16[128,8,1536]{2,1,0:T(8,128)(2,1)}), bf16[128,8,1536]{2,1,0:T(8,128)(2,1)S(1)}, u32[]{:S(2)}, u32[]{:S(2)}) async-start(bf16[128,8,1536]{2,1,0:T(8,128)(2,1)} %bitcast.28), calls=%async_computation.1 | async-start | bytes 6291456 | tf_op jit(solution)/shard_map/all_to_all | solution.py:381
  73.2 5.2 %copy-start.4 = (bf16[384,2048]{1,0:T(8,128)(2,1)S(1)}, bf16[384,2048]{1,0:T(8,128)(2,1)}, u32[]{:S(2)}) copy-start(bf16[384,2048]{1,0:T(8,128)(2,1)} %get-tuple-element.19) | copy-start | bytes 4718596
  73.2 5.2 %copy-start.6 = (bf16[384,768]{1,0:T(8,128)(2,1)S(1)}, bf16[384,768]{1,0:T(8,128)(2,1)}, u32[]{:S(2)}) copy-start(bf16[384,768]{1,0:T(8,128)(2,1)} %get-tuple-element.21) | copy-start | bytes 1769476
  78.4 3.5 %copy-start.3 = (bf16[384,2048]{1,0:T(8,128)(2,1)S(1)}, bf16[384,2048]{1,0:T(8,128)(2,1)}, u32[]{:S(2)}) copy-start(bf16[384,2048]{1,0:T(8,128)(2,1)} %get-tuple-element.23) | copy-start | bytes 4718596
  78.4 3.5 %copy-start.5 = (bf16[384,768]{1,0:T(8,128)(2,1)S(1)}, bf16[384,768]{1,0:T(8,128)(2,1)}, u32[]{:S(2)}) copy-start(bf16[384,768]{1,0:T(8,128)(2,1)} %get-tuple-element.22) | copy-start | bytes 1769476

commit v3 on v2

v3 whole, which is shorter than its diff:
```python
import jax
import jax.numpy as jnp
from jax import lax
from jax.experimental import pallas as pl
from jax.experimental.pallas import tpu as pltpu
from jax.sharding import PartitionSpec as P

CAP = 3
MAIN = 1536
TAIL = 512
WIDTH = MAIN + TAIL
PACK = 8
GROUP = 32
SLAB = PACK * GROUP
SPAN = CAP * GROUP
NT = (((1,), (1,)), ((), ()))
TN = (((0,), (0,)), ((), ()))
ANYWHERE = pl.BlockSpec(memory_space=pl.ANY)
LOCAL = pl.BlockSpec(memory_space=pltpu.VMEM)


def in_hbm(array):
    return pltpu.with_memory_space_constraint(array, pltpu.HBM)


def in_vmem(array):
    return pltpu.with_memory_space_constraint(array, pltpu.VMEM)


def iota(shape, dim):
    return lax.broadcasted_iota(jnp.int32, shape, dim)


def dot(left, right):
    return jnp.dot(left, right, preferred_element_type=jnp.float32)


def column_of(row, count):
    wide = jnp.broadcast_to(row, (count, count))
    return jnp.sum(
        jnp.where(iota((count, count), 0) == iota((count, count), 1), wide, 0.0),
        axis=1,
        keepdims=True,
    )


def ranks(index_row, count, axis):
    expert = column_of(index_row, count)
    same = expert == jnp.broadcast_to(index_row, (count, count))
    first, second = iota((count, count), axis), iota((count, count), 1 - axis)
    found = jnp.sum(jnp.where(same & (first < second), 1.0, 0.0), axis=axis, keepdims=True)
    return found, expert


def slot_code(shape, dim):
    slot = iota(shape, dim)
    group = jnp.zeros_like(slot)
    for edge in range(1, shape[dim] // SPAN):
        group = group + (slot >= SPAN * edge).astype(jnp.int32)
    inner = slot - SPAN * group
    rank = (inner >= GROUP).astype(jnp.int32) + (inner >= 2 * GROUP).astype(jnp.int32)
    return (4 * (GROUP * group + inner - GROUP * rank) + rank).astype(jnp.float32)


def split_matrix():
    out, packed = iota((SLAB, SLAB), 0), iota((SLAB, SLAB), 1)
    match = packed == (out & (GROUP - 1)) * PACK + (out >> 5)
    return jnp.where(match, 1.0, 0.0).astype(jnp.bfloat16)


def join_matrix():
    packed, out = iota((SLAB, SLAB), 0), iota((SLAB, SLAB), 1)
    match = packed == (out & (GROUP - 1)) * PACK + (out >> 5)
    return jnp.where(match, 1.0, 0.0).astype(jnp.bfloat16)


def store_stacked(stacked, value, low, which):
    value = value.astype(jnp.bfloat16)
    width = value.shape[1]
    for group in range(value.shape[0] // SPAN):
        base = SLAB * group
        if low < MAIN:
            stacked[base + SPAN * which : base + SPAN * (which + 1), low : low + width] = value[
                SPAN * group : SPAN * (group + 1)
            ]
        else:
            tail = base + 2 * SPAN + GROUP * which
            for rank in range(CAP):
                start = SPAN * group + GROUP * rank
                column = TAIL * rank + low - MAIN
                stacked[tail : tail + GROUP, column : column + width] = value[
                    start : start + GROUP
                ]


def pack(out, stacked):
    matrix = join_matrix()
    for group in range(out.shape[0] // SLAB):
        part = slice(SLAB * group, SLAB * (group + 1))
        for low in range(0, MAIN, TAIL):
            block = slice(low, low + TAIL)
            out[part, block] = dot(matrix, stacked[part, block]).astype(jnp.bfloat16)


def unpack(packed, matrix, first, second, group):
    base = SPAN * group
    for rank in range(CAP):
        block = slice(TAIL * rank, TAIL * (rank + 1))
        part = dot(matrix, packed[SLAB * group : SLAB * (group + 1), block]).astype(jnp.bfloat16)
        first[base : base + SPAN, block] = part[0:SPAN]
        second[base : base + SPAN, block] = part[SPAN : 2 * SPAN]
        low = base + GROUP * rank
        first[low : low + GROUP, MAIN:] = part[2 * SPAN : 2 * SPAN + GROUP]
        second[low : low + GROUP, MAIN:] = part[2 * SPAN + GROUP :]


def dispatch_kernel(
    index_hbm, weight_hbm, rows_hbm, cot_hbm, out, index, weight, rows, cot, stacked, in_sem
):
    count = rows.shape[0]
    slots = out.shape[0] // PACK * CAP
    loads = [
        pltpu.make_async_copy(source, target, in_sem.at[number])
        for number, (source, target) in enumerate(
            ((index_hbm, index), (weight_hbm, weight), (rows_hbm, rows), (cot_hbm, cot))
        )
    ]
    for load in loads:
        load.start()
    loads[0].wait()
    index_row = index[...].astype(jnp.float32)
    rank_row, _ = ranks(index_row, count, 0)
    place = jnp.where(slot_code((slots, 1), 0) == 4.0 * index_row + rank_row, 1.0, 0.0).astype(
        jnp.bfloat16
    )
    loads[1].wait()
    scale = column_of(weight[...], count)
    loads[2].wait()
    for low in range(0, WIDTH, TAIL):
        store_stacked(stacked, dot(place, rows[:, low : low + TAIL]), low, 0)
    loads[3].wait()
    for low in range(0, WIDTH, TAIL):
        grad = (scale * cot[:, low : low + TAIL].astype(jnp.float32)).astype(jnp.bfloat16)
        store_stacked(stacked, dot(place, grad), low, 1)
    pack(out, stacked)


def dispatch(index, weight, rows, cot, devices):
    count = rows.shape[0]
    return pl.pallas_call(
        dispatch_kernel,
        in_specs=[ANYWHERE] * 4,
        out_specs=LOCAL,
        out_shape=pltpu.VMEM((devices * PACK, MAIN), jnp.bfloat16),
        scratch_shapes=[
            pltpu.VMEM((1, count), jnp.int32),
            pltpu.VMEM((1, count), jnp.float32),
            pltpu.VMEM((count, WIDTH), jnp.bfloat16),
            pltpu.VMEM((count, WIDTH), jnp.bfloat16),
            pltpu.VMEM((devices * PACK, MAIN), jnp.bfloat16),
            pltpu.SemaphoreType.DMA((4,)),
        ],
        compiler_params=pltpu.CompilerParams(vmem_limit_bytes=24 << 20),
        name="dispatch",
    )(in_hbm(index), in_hbm(weight), in_hbm(rows), in_hbm(cot))


def saver(semaphores):
    saves = []

    def save(source, target):
        copy = pltpu.make_async_copy(source, target, semaphores.at[len(saves)])
        copy.start()
        saves.append(copy)

    return save, saves


def expert_kernel(
    got,
    w_gate,
    w_up,
    w_down,
    send_hbm,
    rows_hbm,
    grad_hbm,
    hidden_hbm,
    gate_hbm,
    up_hbm,
    send,
    rows,
    grad,
    hidden,
    gate_pre,
    up_pre,
    stacked,
    out_sem,
):
    save, saves = saver(out_sem)
    groups = got.shape[0] // SLAB
    matrix, join = split_matrix(), join_matrix()
    for group in range(groups):
        unpack(got, matrix, rows, grad, group)
    save(rows, rows_hbm)
    save(grad, grad_hbm)

    gate_act = dot(rows[...], w_gate[...])
    up_act = dot(rows[...], w_up[...])
    hidden_grad = lax.dot_general(
        grad[...], w_down[...], NT, preferred_element_type=jnp.float32
    )
    sigma = jax.nn.sigmoid(gate_act)
    silu_gate = gate_act * sigma
    hidden[...] = (silu_gate * up_act).astype(jnp.bfloat16)
    gate_pre[...] = (
        hidden_grad * up_act * sigma * (1.0 + gate_act * (1.0 - sigma))
    ).astype(jnp.bfloat16)
    up_pre[...] = (hidden_grad * silu_gate).astype(jnp.bfloat16)
    save(hidden, hidden_hbm)
    save(gate_pre, gate_hbm)
    save(up_pre, up_hbm)

    def project(low):
        block = slice(low, low + TAIL)
        store_stacked(stacked, dot(hidden[...], w_down[:, block]), low, 0)
        value = lax.dot_general(
            gate_pre[...], w_gate[block, :], NT, preferred_element_type=jnp.float32
        ) + lax.dot_general(
            up_pre[...], w_up[block, :], NT, preferred_element_type=jnp.float32
        )
        store_stacked(stacked, value, low, 1)

    project(MAIN)
    for rank in range(CAP):
        project(TAIL * rank)
        block = slice(TAIL * rank, TAIL * (rank + 1))
        for group in range(groups):
            part = slice(SLAB * group, SLAB * (group + 1))
            send[part, block] = dot(join, stacked[part, block]).astype(jnp.bfloat16)
        save(send.at[:, block], send_hbm.at[:, block])
    for copy in saves:
        copy.wait()


def expert(got, w_gate, w_up, w_down):
    slots = got.shape[0] // PACK * CAP
    units = w_gate.shape[1]
    shapes = [got.shape] + [(slots, WIDTH)] * 2 + [(slots, units)] * 3
    return pl.pallas_call(
        expert_kernel,
        in_specs=[LOCAL] * 4,
        out_specs=[ANYWHERE] * 6,
        out_shape=[pltpu.HBM(shape, jnp.bfloat16) for shape in shapes],
        scratch_shapes=[pltpu.VMEM(shape, jnp.bfloat16) for shape in shapes]
        + [
            pltpu.VMEM(got.shape, jnp.bfloat16),
            pltpu.SemaphoreType.DMA((5 + CAP,)),
        ],
        compiler_params=pltpu.CompilerParams(vmem_limit_bytes=40 << 20),
        cost_estimate=pl.CostEstimate(
            flops=12 * slots * WIDTH * units,
            bytes_accessed=4 * got.size + 6 * WIDTH * units + 4 * slots * WIDTH,
            transcendentals=slots * units,
        ),
        name="expert",
    )(in_vmem(got), in_vmem(w_gate), in_vmem(w_up), in_vmem(w_down))


def gradient_kernel(
    index,
    weight,
    rows,
    grad,
    hidden,
    gate_pre,
    up_pre,
    gate_hbm,
    up_hbm,
    down_hbm,
    pick,
    scale,
    gate_grad,
    up_grad,
    down_grad,
    out_sem,
):
    count = index.shape[1]
    slots = rows.shape[0]
    save, saves = saver(out_sem)

    for left, right, result, target in (
        (rows, gate_pre, gate_grad, gate_hbm),
        (rows, up_pre, up_grad, up_hbm),
        (hidden, grad, down_grad, down_hbm),
    ):
        for low in range(0, left.shape[1], 256):
            block = slice(low, low + 256)
            result[block, :] = lax.dot_general(
                left[:, block], right[...], TN, preferred_element_type=jnp.float32
            ).astype(jnp.bfloat16)
        save(result, target)
    rank, expert_column = ranks(index[...].astype(jnp.float32), count, 1)
    code = 4.0 * expert_column + rank
    pick[...] = jnp.where(code == slot_code((1, slots), 1), 1.0, 0.0).astype(jnp.bfloat16)
    scale[...] = jnp.broadcast_to(column_of(weight[...], count), scale.shape)
    for copy in saves:
        copy.wait()


def gradients(index, weight, rows, grad, hidden, gate_pre, up_pre):
    count = index.shape[1]
    slots, units = hidden.shape
    tall = (WIDTH, units)
    flat = (units, WIDTH)
    return pl.pallas_call(
        gradient_kernel,
        in_specs=[LOCAL] * 7,
        out_specs=[ANYWHERE] * 3 + [LOCAL] * 2,
        out_shape=[
            pltpu.HBM(tall, jnp.bfloat16),
            pltpu.HBM(tall, jnp.bfloat16),
            pltpu.HBM(flat, jnp.bfloat16),
            pltpu.VMEM((count, slots), jnp.bfloat16),
            pltpu.VMEM((count, 128), jnp.float32),
        ],
        scratch_shapes=[
            pltpu.VMEM(tall, jnp.bfloat16),
            pltpu.VMEM(tall, jnp.bfloat16),
            pltpu.VMEM(flat, jnp.bfloat16),
            pltpu.SemaphoreType.DMA((3,)),
        ],
        compiler_params=pltpu.CompilerParams(vmem_limit_bytes=40 << 20),
        cost_estimate=pl.CostEstimate(
            flops=6 * slots * WIDTH * units,
            bytes_accessed=6 * WIDTH * units + 4 * slots * WIDTH,
            transcendentals=0,
        ),
        name="gradients",
    )(
        in_hbm(index),
        in_hbm(weight),
        in_hbm(rows),
        in_hbm(grad),
        in_hbm(hidden),
        in_hbm(gate_pre),
        in_hbm(up_pre),
    )


def combine_kernel(
    pick,
    scale,
    cot_hbm,
    got,
    out_hbm,
    row_hbm,
    wgrad_hbm,
    cot,
    first,
    second,
    out,
    row,
    wgrad,
    in_sem,
    out_sem,
):
    count = cot.shape[0]
    load = pltpu.make_async_copy(cot_hbm, cot, in_sem)
    load.start()
    matrix = split_matrix()
    for group in range(got.shape[0] // SLAB):
        unpack(got, matrix, first, second, group)
    save, saves = saver(out_sem)
    factor = scale[:, 0:1]
    total = jnp.zeros((count, 1), jnp.float32)

    def store_rows(block):
        row[:, block] = dot(pick[...], second[:, block]).astype(jnp.bfloat16)
        save(row.at[:, block], row_hbm.at[:, block])

    blocks = [slice(low, low + TAIL) for low in range(0, WIDTH, TAIL)]
    for block in blocks:
        if block != blocks[-1]:
            store_rows(block)
        value = dot(pick[...], first[:, block])
        out[:, block] = (factor * value).astype(jnp.bfloat16)
        save(out.at[:, block], out_hbm.at[:, block])
        if block == blocks[0]:
            load.wait()
        total += jnp.sum(cot[:, block].astype(jnp.float32) * value, axis=1, keepdims=True)
    eye = iota((count, count), 0) == iota((count, count), 1)
    wgrad[...] = jnp.sum(jnp.where(eye, total, 0.0), axis=0, keepdims=True)
    save(wgrad, wgrad_hbm)
    store_rows(blocks[-1])
    for copy in saves:
        copy.wait()


def combine(pick, scale, cot, got):
    count = cot.shape[0]
    slots = got.shape[0] // PACK * CAP
    return pl.pallas_call(
        combine_kernel,
        in_specs=[LOCAL, LOCAL, ANYWHERE, LOCAL],
        out_specs=[ANYWHERE] * 3,
        out_shape=[
            pltpu.HBM((count, WIDTH), jnp.bfloat16),
            pltpu.HBM((count, WIDTH), jnp.bfloat16),
            pltpu.HBM((1, count), jnp.float32),
        ],
        scratch_shapes=[
            pltpu.VMEM((count, WIDTH), jnp.bfloat16),
            pltpu.VMEM((slots, WIDTH), jnp.bfloat16),
            pltpu.VMEM((slots, WIDTH), jnp.bfloat16),
            pltpu.VMEM((count, WIDTH), jnp.bfloat16),
            pltpu.VMEM((count, WIDTH), jnp.bfloat16),
            pltpu.VMEM((1, count), jnp.float32),
            pltpu.SemaphoreType.DMA,
            pltpu.SemaphoreType.DMA((2 * WIDTH // TAIL + 1,)),
        ],
        compiler_params=pltpu.CompilerParams(vmem_limit_bytes=24 << 20),
        name="combine",
    )(in_vmem(pick), in_vmem(scale), in_hbm(cot), in_vmem(got))


def exchange(packed, devices):
    moved = lax.all_to_all(
        packed.reshape(devices, PACK, MAIN), "expert", split_axis=0, concat_axis=0, tiled=True
    )
    return moved.reshape(packed.shape)


def local(routed_rows, expert_index, route_weight, cotangent, gate_weight, up_weight, down_weight):
    devices = lax.axis_size("expert")
    count = routed_rows.shape[0]
    index = expert_index.reshape(1, count)
    weight = route_weight.reshape(1, count)
    packed = dispatch(index, weight, routed_rows, cotangent, devices)
    got = exchange(packed, devices)
    send, *saved = expert(got, gate_weight[0], up_weight[0], down_weight[0])
    back = exchange(send, devices)
    gate_grad, up_grad, down_grad, pick, scale = gradients(index, weight, *saved)
    layer_out, row_grad, weight_grad = combine(pick, scale, cotangent, back)
    return (
        layer_out,
        row_grad,
        weight_grad.reshape(count),
        gate_grad[None],
        up_grad[None],
        down_grad[None],
    )


def solution(mesh):
    rows = P("expert", None)
    weights = P("expert", None, None)
    return jax.shard_map(
        local,
        mesh=mesh,
        in_specs=(rows, rows, P("expert"), rows, weights, weights, weights),
        out_specs=(rows, rows, P("expert"), weights, weights, weights),
        check_vma=False,
    )
```

time: 120 us -> 117 us (0.975)
  matrix products: 12.2 us -> 0 us
  Pallas kernels: 19 us -> 25.9 us
  waiting for transfers between devices: 29.6 us -> 32.6 us
    dot_general x3 -> x0, matrix products: 12.2 us -> none  [weight_product(): lax.dot_general(left, right, TN, preferred_element_type=jnp.float32)]
    pallas_call x1 -> x2, Pallas kernels: 4.28 us -> 12 us  [the longest x1 9.19 us: gradients(): pl.pallas_call(gradient_kernel, in_specs=[LOCAL] * 7, out_specs=[ANYWHERE...]
    all_to_all x1, waiting for transfers between devices: 29.6 us -> 32.6 us  [exchange(): lax.all_to_all(packed.reshape(devices, PACK, MAIN), 'expert', split_axis=...]
  transfers between devices with their start and end apart: 1 -> 1, of which waited for: 1 -> 1; matrix products, arithmetic and copies ran while one was open for 10% -> 0% of each run, Pallas kernels for 0% -> 8%
where the time goes in v3:
time: 117 us
  blocking collectives  53 us (45%)
  waiting for transfers between devices  32.6 us (28%)
  Pallas kernels  25.9 us (22%)
  starting transfers between devices  4.59 us (4%)
    all_to_all x1, blocking collectives, exchange(): lax.all_to_all(packed.reshape(devices, PACK, MAIN), 'expert', split_axis=...  53 us
    all_to_all x1, waiting for transfers between devices, exchange(): lax.all_to_all(packed.reshape(devices, PACK, MAIN), 'expert', split_axis=...  32.6 us
    pallas_call x1, Pallas kernels, expert(): pl.pallas_call(expert_kernel, in_specs=[LOCAL] * 4, out_specs=[ANYWHERE]...  10.6 us
    pallas_call x1, Pallas kernels, gradients(): pl.pallas_call(gradient_kernel, in_specs=[LOCAL] * 7, out_specs=[ANYWHERE...  9.19 us
    all_to_all x1, starting transfers between devices, exchange(): lax.all_to_all(packed.reshape(devices, PACK, MAIN), 'expert', split_axis=...  4.59 us
    pallas_call x1, Pallas kernels, dispatch(): pl.pallas_call(dispatch_kernel, in_specs=[ANYWHERE] * 4, out_specs=LOCAL,...  3.36 us
    pallas_call x1, Pallas kernels, combine(): pl.pallas_call(combine_kernel, in_specs=[LOCAL, LOCAL, ANYWHERE, LOCAL],...  2.76 us
  transfers between devices with their start and end apart: 1, of which 1 were waited for; matrix products, arithmetic and copies ran while one was open for 0% of the time, Pallas kernels for 8%

profile of v3, /device:TPU:1, one launch (start us, length us, event | category | flops | bytes accessed | tf_op | source)
XLA Modules:
  0.0 117.0 jit_solution(4631338558974545347)
XLA Ops:
  0.6 0.0 copy-start.2
  0.6 3.4 %dispatch.1 = bf16[1024,1536]{1,0:T(8,128)(2,1)S(1)} custom-call(s32[1,192]{1,0:T(1,128)} %bitcast.20, f32[1,192]{1,0:T(1,128)} %bitcast.22, bf16[192,2048]{1,0:T(8,128)(2,1)} %rows_hbm.1, bf16[192,2048]{1,0:T(8,128)(2,1)} %cot_hbm.3), custom_call_target="tpu_custom_call" | custom-call | tf_op jit(solution)/shard_map/dispatch/pallas_call | solution.py:150
  4.0 0.0 copy-start
  4.0 0.0 copy-start.1
  4.0 53.0 %all_to_all.10 = bf16[128,8,1536]{2,1,0:T(8,128)(2,1)S(1)} all-to-all(bf16[128,8,1536]{2,1,0:T(8,128)(2,1)S(1)} %bitcast.14), channel_id=1, replica_groups=mesh['expert'=128] {'expert'}, dimensions={0} | all-to-all | bytes 6291456 | tf_op jit(solution)/shard_map/all_to_all | solution.py:427
  57.0 0.0 copy-done.2
  57.0 0.0 copy-done
  57.0 0.0 copy-done.1
  57.0 10.6 %expert.1 = (bf16[1024,1536]{1,0:T(8,128)(2,1)}, bf16[384,2048]{1,0:T(8,128)(2,1)}, bf16[384,2048]{1,0:T(8,128)(2,1)}, bf16[384,768]{1,0:T(8,128)(2,1)}, bf16[38...) custom-call(bf16[1024,1536]{1,0:T(8,128)(2,1)S(1)} %bitcast.15, bf16[2048,768]{1,0:T(8,128)(2,1)S(1)} %bitcast.16, ...), custom_call_target="tpu_custom_call" | custom-call | flops 7247757312 | bytes 18874368 | tf_op jit(solution)/shard_map/expert/pallas_call | solution.py:249
  67.7 4.6 %all-to-all-start.1 = ((bf16[128,8,1536]{2,1,0:T(8,128)(2,1)}), bf16[128,8,1536]{2,1,0:T(8,128)(2,1)S(1)}, u32[]{:S(2)}, u32[]{:S(2)}) async-start(bf16[128,8,1536]{2,1,0:T(8,128)(2,1)} %bitcast.19), calls=%async_computation.1 | async-start | bytes 6291456 | tf_op jit(solution)/shard_map/all_to_all | solution.py:427
  72.2 9.2 %gradients.1 = (bf16[2048,768]{1,0:T(8,128)(2,1)}, bf16[2048,768]{1,0:T(8,128)(2,1)}, bf16[768,2048]{1,0:T(8,128)(2,1)}, bf16[192,384]{1,0:T(8,128)(2,1)S(1)}, f32[192,128]{1,0:T(8,128)S(1)}) custom-call(s32[1,192]{1,0:T(1,128)} %bitcast.21, f32[1,192]{1,0:T(1,128)} %bitcast.23, bf16[384,2048]{1,0:T(8,128)(2,1)} %get-tuple-element.20.rows, ...), custom_call_target="tpu_custom_call" | custom-call | flops 3623878656 | bytes 12582912 | tf_op jit(solution)/shard_map/gradients/pallas_call | solution.py:315
  81.4 32.6 %all-to-all-done.1 = bf16[128,8,1536]{2,1,0:T(8,128)(2,1)S(1)} async-done(((bf16[128,8,1536]{2,1,0:T(8,128)(2,1)}), bf16[128,8,1536]{2,1,0:T(8,128)(2,1)S(1)}, u32[]{:S(2)}, u32[]{:S(2)}) %all-to-all-start.1) | async-done | bytes 3145760 | tf_op jit(solution)/shard_map/all_to_all | solution.py:427
  114.1 2.8 %combine.1 = (bf16[192,2048]{1,0:T(8,128)(2,1)}, bf16[192,2048]{1,0:T(8,128)(2,1)}, f32[1,192]{1,0:T(1,128)}) custom-call(bf16[192,384]{1,0:T(8,128)(2,1)S(1)} %get-tuple-element.25.pick, f32[192,128]{1,0:T(8,128)S(1)} %get-tuple-element.26.scale, bf16[192,2048]{1,0:T(8,128)(2,1)} %cot_hbm.3, bf16[1024,1536]{1,0:T(8,128)(2,1)S(1)} %bitcast.13), custom_call_target="tpu_custom_call" | custom-call | tf_op jit(solution)/shard_map/combine/pallas_call | solution.py:402
Async XLA Ops:
  0.6 56.4 %copy-start.2 = (bf16[1,768,2048]{2,1,0:T(8,128)(2,1)S(1)}, bf16[1,768,2048]{2,1,0:T(8,128)(2,1)}, u32[]{:S(2)}) copy-start(bf16[1,768,2048]{2,1,0:T(8,128)(2,1)} %param.13) | copy-start | bytes 9437188
  4.0 53.0 %copy-start = (bf16[1,2048,768]{2,1,0:T(8,128)(2,1)S(1)}, bf16[1,2048,768]{2,1,0:T(8,128)(2,1)}, u32[]{:S(2)}) copy-start(bf16[1,2048,768]{2,1,0:T(8,128)(2,1)} %param.11) | copy-start | bytes 9437188
  4.0 53.0 %copy-start.1 = (bf16[1,2048,768]{2,1,0:T(8,128)(2,1)S(1)}, bf16[1,2048,768]{2,1,0:T(8,128)(2,1)}, u32[]{:S(2)}) copy-start(bf16[1,2048,768]{2,1,0:T(8,128)(2,1)} %param.12) | copy-start | bytes 9437188
  67.7 46.4 %all-to-all-start.1 = ((bf16[128,8,1536]{2,1,0:T(8,128)(2,1)}), bf16[128,8,1536]{2,1,0:T(8,128)(2,1)S(1)}, u32[]{:S(2)}, u32[]{:S(2)}) async-start(bf16[128,8,1536]{2,1,0:T(8,128)(2,1)} %bitcast.19), calls=%async_computation.1 | async-start | bytes 6291456 | tf_op jit(solution)/shard_map/all_to_all | solution.py:427

commit v4 on v3

--- a/solution.py
+++ b/solution.py
@@ -136,12 +136,13 @@
     loads[1].wait()
     scale = column_of(weight[...], count)
     loads[2].wait()
-    for low in range(0, WIDTH, TAIL):
-        store_stacked(stacked, dot(place, rows[:, low : low + TAIL]), low, 0)
+    blocks = [slice(0, MAIN), slice(MAIN, WIDTH)]
+    for block in blocks:
+        store_stacked(stacked, dot(place, rows[:, block]), block.start, 0)
     loads[3].wait()
-    for low in range(0, WIDTH, TAIL):
-        grad = (scale * cot[:, low : low + TAIL].astype(jnp.float32)).astype(jnp.bfloat16)
-        store_stacked(stacked, dot(place, grad), low, 1)
+    for block in blocks:
+        grad = (scale * cot[:, block].astype(jnp.float32)).astype(jnp.bfloat16)
+        store_stacked(stacked, dot(place, grad), block.start, 1)
     pack(out, stacked)
 
 
@@ -237,7 +238,10 @@
         for group in range(groups):
             part = slice(SLAB * group, SLAB * (group + 1))
             send[part, block] = dot(join, stacked[part, block]).astype(jnp.bfloat16)
-        save(send.at[:, block], send_hbm.at[:, block])
+        pieces = 1 if rank < CAP - 1 else 2
+        for piece in range(pieces):
+            part = pl.ds(send.shape[0] // pieces * piece, send.shape[0] // pieces)
+            save(send.at[part, block], send_hbm.at[part, block])
     for copy in saves:
         copy.wait()
 
@@ -254,7 +258,7 @@
         scratch_shapes=[pltpu.VMEM(shape, jnp.bfloat16) for shape in shapes]
         + [
             pltpu.VMEM(got.shape, jnp.bfloat16),
-            pltpu.SemaphoreType.DMA((5 + CAP,)),
+            pltpu.SemaphoreType.DMA((6 + CAP,)),
         ],
         compiler_params=pltpu.CompilerParams(vmem_limit_bytes=40 << 20),
         cost_estimate=pl.CostEstimate(

time: 117 us -> 117 us (level)
  no operation moved by 1% of the time
where the time goes in v4:
time: 117 us
  blocking collectives  53 us (45%)
  waiting for transfers between devices  32.6 us (28%)
  Pallas kernels  25.9 us (22%)
  starting transfers between devices  4.59 us (4%)
    all_to_all x1, blocking collectives, exchange(): lax.all_to_all(packed.reshape(devices, PACK, MAIN), 'expert', split_axis=...  53 us
    all_to_all x1, waiting for transfers between devices, exchange(): lax.all_to_all(packed.reshape(devices, PACK, MAIN), 'expert', split_axis=...  32.6 us
    pallas_call x1, Pallas kernels, expert(): pl.pallas_call(expert_kernel, in_specs=[LOCAL] * 4, out_specs=[ANYWHERE]...  10.6 us
    pallas_call x1, Pallas kernels, gradients(): pl.pallas_call(gradient_kernel, in_specs=[LOCAL] * 7, out_specs=[ANYWHERE...  9.19 us
    all_to_all x1, starting transfers between devices, exchange(): lax.all_to_all(packed.reshape(devices, PACK, MAIN), 'expert', split_axis=...  4.59 us
    pallas_call x1, Pallas kernels, dispatch(): pl.pallas_call(dispatch_kernel, in_specs=[ANYWHERE] * 4, out_specs=LOCAL,...  3.36 us
    pallas_call x1, Pallas kernels, combine(): pl.pallas_call(combine_kernel, in_specs=[LOCAL, LOCAL, ANYWHERE, LOCAL],...  2.76 us
  transfers between devices with their start and end apart: 1, of which 1 were waited for; matrix products, arithmetic and copies ran while one was open for 0% of the time, Pallas kernels for 8%

profile of v4, /device:TPU:1, one launch (start us, length us, event | category | flops | bytes accessed | tf_op | source)
XLA Modules:
  0.0 117.0 jit_solution(38075296650857854)
XLA Ops:
  0.6 0.0 copy-start.2
  0.6 3.4 %dispatch.1 = bf16[1024,1536]{1,0:T(8,128)(2,1)S(1)} custom-call(s32[1,192]{1,0:T(1,128)} %bitcast.20, f32[1,192]{1,0:T(1,128)} %bitcast.22, bf16[192,2048]{1,0:T(8,128)(2,1)} %rows_hbm.1, bf16[192,2048]{1,0:T(8,128)(2,1)} %cot_hbm.3), custom_call_target="tpu_custom_call" | custom-call | tf_op jit(solution)/shard_map/dispatch/pallas_call | solution.py:151
  4.0 0.0 copy-start
  4.0 0.0 copy-start.1
  4.0 53.0 %all_to_all.10 = bf16[128,8,1536]{2,1,0:T(8,128)(2,1)S(1)} all-to-all(bf16[128,8,1536]{2,1,0:T(8,128)(2,1)S(1)} %bitcast.14), channel_id=1, replica_groups=mesh['expert'=128] {'expert'}, dimensions={0} | all-to-all | bytes 6291456 | tf_op jit(solution)/shard_map/all_to_all | solution.py:431
  57.0 0.0 copy-done.2
  57.0 0.0 copy-done
  57.0 0.0 copy-done.1
  57.0 10.6 %expert.1 = (bf16[1024,1536]{1,0:T(8,128)(2,1)}, bf16[384,2048]{1,0:T(8,128)(2,1)}, bf16[384,2048]{1,0:T(8,128)(2,1)}, bf16[384,768]{1,0:T(8,128)(2,1)}, bf16[38...) custom-call(bf16[1024,1536]{1,0:T(8,128)(2,1)S(1)} %bitcast.15, bf16[2048,768]{1,0:T(8,128)(2,1)S(1)} %bitcast.16, ...), custom_call_target="tpu_custom_call" | custom-call | flops 7247757312 | bytes 18874368 | tf_op jit(solution)/shard_map/expert/pallas_call | solution.py:253
  67.7 4.6 %all-to-all-start.1 = ((bf16[128,8,1536]{2,1,0:T(8,128)(2,1)}), bf16[128,8,1536]{2,1,0:T(8,128)(2,1)S(1)}, u32[]{:S(2)}, u32[]{:S(2)}) async-start(bf16[128,8,1536]{2,1,0:T(8,128)(2,1)} %bitcast.19), calls=%async_computation.1 | async-start | bytes 6291456 | tf_op jit(solution)/shard_map/all_to_all | solution.py:431
  72.3 9.2 %gradients.1 = (bf16[2048,768]{1,0:T(8,128)(2,1)}, bf16[2048,768]{1,0:T(8,128)(2,1)}, bf16[768,2048]{1,0:T(8,128)(2,1)}, bf16[192,384]{1,0:T(8,128)(2,1)S(1)}, f32[192,128]{1,0:T(8,128)S(1)}) custom-call(s32[1,192]{1,0:T(1,128)} %bitcast.21, f32[1,192]{1,0:T(1,128)} %bitcast.23, bf16[384,2048]{1,0:T(8,128)(2,1)} %get-tuple-element.20.rows, ...), custom_call_target="tpu_custom_call" | custom-call | flops 3623878656 | bytes 12582912 | tf_op jit(solution)/shard_map/gradients/pallas_call | solution.py:319
  81.5 32.6 %all-to-all-done.1 = bf16[128,8,1536]{2,1,0:T(8,128)(2,1)S(1)} async-done(((bf16[128,8,1536]{2,1,0:T(8,128)(2,1)}), bf16[128,8,1536]{2,1,0:T(8,128)(2,1)S(1)}, u32[]{:S(2)}, u32[]{:S(2)}) %all-to-all-start.1) | async-done | bytes 3145760 | tf_op jit(solution)/shard_map/all_to_all | solution.py:431
  114.1 2.8 %combine.1 = (bf16[192,2048]{1,0:T(8,128)(2,1)}, bf16[192,2048]{1,0:T(8,128)(2,1)}, f32[1,192]{1,0:T(1,128)}) custom-call(bf16[192,384]{1,0:T(8,128)(2,1)S(1)} %get-tuple-element.25.pick, f32[192,128]{1,0:T(8,128)S(1)} %get-tuple-element.26.scale, bf16[192,2048]{1,0:T(8,128)(2,1)} %cot_hbm.3, bf16[1024,1536]{1,0:T(8,128)(2,1)S(1)} %bitcast.13), custom_call_target="tpu_custom_call" | custom-call | tf_op jit(solution)/shard_map/combine/pallas_call | solution.py:406
Async XLA Ops:
  0.6 56.4 %copy-start.2 = (bf16[1,768,2048]{2,1,0:T(8,128)(2,1)S(1)}, bf16[1,768,2048]{2,1,0:T(8,128)(2,1)}, u32[]{:S(2)}) copy-start(bf16[1,768,2048]{2,1,0:T(8,128)(2,1)} %param.13) | copy-start | bytes 9437188
  4.0 53.0 %copy-start = (bf16[1,2048,768]{2,1,0:T(8,128)(2,1)S(1)}, bf16[1,2048,768]{2,1,0:T(8,128)(2,1)}, u32[]{:S(2)}) copy-start(bf16[1,2048,768]{2,1,0:T(8,128)(2,1)} %param.11) | copy-start | bytes 9437188
  4.0 53.0 %copy-start.1 = (bf16[1,2048,768]{2,1,0:T(8,128)(2,1)S(1)}, bf16[1,2048,768]{2,1,0:T(8,128)(2,1)}, u32[]{:S(2)}) copy-start(bf16[1,2048,768]{2,1,0:T(8,128)(2,1)} %param.12) | copy-start | bytes 9437188
  67.7 46.4 %all-to-all-start.1 = ((bf16[128,8,1536]{2,1,0:T(8,128)(2,1)}), bf16[128,8,1536]{2,1,0:T(8,128)(2,1)S(1)}, u32[]{:S(2)}, u32[]{:S(2)}) async-start(bf16[128,8,1536]{2,1,0:T(8,128)(2,1)} %bitcast.19), calls=%async_computation.1 | async-start | bytes 6291456 | tf_op jit(solution)/shard_map/all_to_all | solution.py:431

commit v5 on v4

--- a/solution.py
+++ b/solution.py
@@ -214,7 +214,7 @@
     silu_gate = gate_act * sigma
     hidden[...] = (silu_gate * up_act).astype(jnp.bfloat16)
     gate_pre[...] = (
-        hidden_grad * up_act * sigma * (1.0 + gate_act * (1.0 - sigma))
+        hidden_grad * up_act * (sigma + silu_gate * (1.0 - sigma))
     ).astype(jnp.bfloat16)
     up_pre[...] = (hidden_grad * silu_gate).astype(jnp.bfloat16)
     save(hidden, hidden_hbm)

time: 117 us -> 117 us (level)
  no operation moved by 1% of the time
where the time goes in v5:
time: 117 us
  blocking collectives  53 us (45%)
  waiting for transfers between devices  32.6 us (28%)
  Pallas kernels  25.9 us (22%)
  starting transfers between devices  4.59 us (4%)
    all_to_all x1, blocking collectives, exchange(): lax.all_to_all(packed.reshape(devices, PACK, MAIN), 'expert', split_axis=...  53 us
    all_to_all x1, waiting for transfers between devices, exchange(): lax.all_to_all(packed.reshape(devices, PACK, MAIN), 'expert', split_axis=...  32.6 us
    pallas_call x1, Pallas kernels, expert(): pl.pallas_call(expert_kernel, in_specs=[LOCAL] * 4, out_specs=[ANYWHERE]...  10.6 us
    pallas_call x1, Pallas kernels, gradients(): pl.pallas_call(gradient_kernel, in_specs=[LOCAL] * 7, out_specs=[ANYWHERE...  9.19 us
    all_to_all x1, starting transfers between devices, exchange(): lax.all_to_all(packed.reshape(devices, PACK, MAIN), 'expert', split_axis=...  4.59 us
    pallas_call x1, Pallas kernels, dispatch(): pl.pallas_call(dispatch_kernel, in_specs=[ANYWHERE] * 4, out_specs=LOCAL,...  3.36 us
    pallas_call x1, Pallas kernels, combine(): pl.pallas_call(combine_kernel, in_specs=[LOCAL, LOCAL, ANYWHERE, LOCAL],...  2.77 us
  transfers between devices with their start and end apart: 1, of which 1 were waited for; matrix products, arithmetic and copies ran while one was open for 0% of the time, Pallas kernels for 8%

profile of v5, /device:TPU:1, one launch (start us, length us, event | category | flops | bytes accessed | tf_op | source)
XLA Modules:
  0.0 117.0 jit_solution(8071706334956042006)
XLA Ops:
  0.6 0.0 copy-start.2
  0.6 3.4 %dispatch.1 = bf16[1024,1536]{1,0:T(8,128)(2,1)S(1)} custom-call(s32[1,192]{1,0:T(1,128)} %bitcast.20, f32[1,192]{1,0:T(1,128)} %bitcast.22, bf16[192,2048]{1,0:T(8,128)(2,1)} %rows_hbm.1, bf16[192,2048]{1,0:T(8,128)(2,1)} %cot_hbm.3), custom_call_target="tpu_custom_call" | custom-call | tf_op jit(solution)/shard_map/dispatch/pallas_call | solution.py:151
  4.0 0.0 copy-start
  4.0 0.0 copy-start.1
  4.0 53.0 %all_to_all.10 = bf16[128,8,1536]{2,1,0:T(8,128)(2,1)S(1)} all-to-all(bf16[128,8,1536]{2,1,0:T(8,128)(2,1)S(1)} %bitcast.14), channel_id=1, replica_groups=mesh['expert'=128] {'expert'}, dimensions={0} | all-to-all | bytes 6291456 | tf_op jit(solution)/shard_map/all_to_all | solution.py:431
  57.0 0.0 copy-done.2
  57.0 0.0 copy-done
  57.0 0.0 copy-done.1
  57.0 10.6 %expert.1 = (bf16[1024,1536]{1,0:T(8,128)(2,1)}, bf16[384,2048]{1,0:T(8,128)(2,1)}, bf16[384,2048]{1,0:T(8,128)(2,1)}, bf16[384,768]{1,0:T(8,128)(2,1)}, bf16[38...) custom-call(bf16[1024,1536]{1,0:T(8,128)(2,1)S(1)} %bitcast.15, bf16[2048,768]{1,0:T(8,128)(2,1)S(1)} %bitcast.16, ...), custom_call_target="tpu_custom_call" | custom-call | flops 7247757312 | bytes 18874368 | tf_op jit(solution)/shard_map/expert/pallas_call | solution.py:253
  67.6 4.6 %all-to-all-start.1 = ((bf16[128,8,1536]{2,1,0:T(8,128)(2,1)}), bf16[128,8,1536]{2,1,0:T(8,128)(2,1)S(1)}, u32[]{:S(2)}, u32[]{:S(2)}) async-start(bf16[128,8,1536]{2,1,0:T(8,128)(2,1)} %bitcast.19), calls=%async_computation.1 | async-start | bytes 6291456 | tf_op jit(solution)/shard_map/all_to_all | solution.py:431
  72.2 9.2 %gradients.1 = (bf16[2048,768]{1,0:T(8,128)(2,1)}, bf16[2048,768]{1,0:T(8,128)(2,1)}, bf16[768,2048]{1,0:T(8,128)(2,1)}, bf16[192,384]{1,0:T(8,128)(2,1)S(1)}, f32[192,128]{1,0:T(8,128)S(1)}) custom-call(s32[1,192]{1,0:T(1,128)} %bitcast.21, f32[1,192]{1,0:T(1,128)} %bitcast.23, bf16[384,2048]{1,0:T(8,128)(2,1)} %get-tuple-element.20.rows, ...), custom_call_target="tpu_custom_call" | custom-call | flops 3623878656 | bytes 12582912 | tf_op jit(solution)/shard_map/gradients/pallas_call | solution.py:319
  81.4 32.6 %all-to-all-done.1 = bf16[128,8,1536]{2,1,0:T(8,128)(2,1)S(1)} async-done(((bf16[128,8,1536]{2,1,0:T(8,128)(2,1)}), bf16[128,8,1536]{2,1,0:T(8,128)(2,1)S(1)}, u32[]{:S(2)}, u32[]{:S(2)}) %all-to-all-start.1) | async-done | bytes 3145760 | tf_op jit(solution)/shard_map/all_to_all | solution.py:431
  114.0 2.8 %combine.1 = (bf16[192,2048]{1,0:T(8,128)(2,1)}, bf16[192,2048]{1,0:T(8,128)(2,1)}, f32[1,192]{1,0:T(1,128)}) custom-call(bf16[192,384]{1,0:T(8,128)(2,1)S(1)} %get-tuple-element.25.pick, f32[192,128]{1,0:T(8,128)S(1)} %get-tuple-element.26.scale, bf16[192,2048]{1,0:T(8,128)(2,1)} %cot_hbm.3, bf16[1024,1536]{1,0:T(8,128)(2,1)S(1)} %bitcast.13), custom_call_target="tpu_custom_call" | custom-call | tf_op jit(solution)/shard_map/combine/pallas_call | solution.py:406
Async XLA Ops:
  0.6 56.4 %copy-start.2 = (bf16[1,768,2048]{2,1,0:T(8,128)(2,1)S(1)}, bf16[1,768,2048]{2,1,0:T(8,128)(2,1)}, u32[]{:S(2)}) copy-start(bf16[1,768,2048]{2,1,0:T(8,128)(2,1)} %param.13) | copy-start | bytes 9437188
  4.0 53.0 %copy-start = (bf16[1,2048,768]{2,1,0:T(8,128)(2,1)S(1)}, bf16[1,2048,768]{2,1,0:T(8,128)(2,1)}, u32[]{:S(2)}) copy-start(bf16[1,2048,768]{2,1,0:T(8,128)(2,1)} %param.11) | copy-start | bytes 9437188
  4.0 53.0 %copy-start.1 = (bf16[1,2048,768]{2,1,0:T(8,128)(2,1)S(1)}, bf16[1,2048,768]{2,1,0:T(8,128)(2,1)}, u32[]{:S(2)}) copy-start(bf16[1,2048,768]{2,1,0:T(8,128)(2,1)} %param.12) | copy-start | bytes 9437188
  67.6 46.4 %all-to-all-start.1 = ((bf16[128,8,1536]{2,1,0:T(8,128)(2,1)}), bf16[128,8,1536]{2,1,0:T(8,128)(2,1)S(1)}, u32[]{:S(2)}, u32[]{:S(2)}) async-start(bf16[128,8,1536]{2,1,0:T(8,128)(2,1)} %bitcast.19), calls=%async_computation.1 | async-start | bytes 6291456 | tf_op jit(solution)/shard_map/all_to_all | solution.py:431
